TPU v7x, 256 devices: a whole 4x4x8 slice. The times are simulated.
256 devices in a mesh: rows: 8 (over z), vocab: 32 (over y, x, core).
Axes of the slice: x: 4, y: 4, z: 8, core: 2. Of those that a mesh axis runs over, the one named last changes fastest.
Arguments:
- hidden: bfloat16 [1024, 8192], P('rows', 'vocab'), may hold values from -30 to 30
- head: bfloat16 [8192, 152064], P(None, ('vocab', 'rows')), may hold values from -1 to 1
- states: int32 [1024], replicated, may hold values from 0 to 2047
- class_of: int32 [152064], P('vocab'), may hold values from 0 to 255, as said below
- table: int32 [2048, 8], replicated, may hold values from -2147483648 to 2147483646, as said below
Outputs:
- log_probs: float32 [1024, 152064], P('rows', 'vocab')
- entropy: float32 [1024], P('rows')
Inputs may be any that keep to these rules, and one draw needn't show every extreme that they name: `class_of`: class 0 is the class of at least one token. `table`: bit 0 of word 0 is set in every state, so class 0 is allowed everywhere.
All inputs are finite; a program needn't handle non-finite values.
Results may differ from a plain program's by a relative error of at most 0.0003.
Values may be sent and summed in bfloat16 or wider, within the bound.
No kernel may reach another device: no remote copies, remote signals or barrier semaphores. Data moves between devices by JAX's collectives and lax.ppermute only.
A program may use at most 128 MiB of HBM per device.

v0:
```python
import functools

import jax
import jax.numpy as jnp
from jax import lax
from jax.experimental import pallas as pl
from jax.experimental.pallas import tpu as pltpu
from jax.sharding import PartitionSpec as P

masked_floor = -1e30
side = 4
levels = 65520.0
vmem_bytes = 24 * 2**20
padded = 608
far_offsets = (4, 3, -3, 2)
near_offsets = (-2, -1, 1, 0)


def plane_shift(lead, step):
    pairs = []
    for y in range(side):
        for x in range(side):
            for core in range(2):
                along_x = (core == 0) == lead
                to_y = y if along_x else (y + step) % side
                to_x = (x + step) % side if along_x else x
                pairs.append(((y * side + x) * 2 + core, (to_y * side + to_x) * 2 + core))
    return pairs


def sent(block, pairs):
    return lax.ppermute(block, "vocab", pairs)


def from_row_group(block, offset):
    count = lax.axis_size("rows")
    return lax.ppermute(block, "rows", [((k + offset) % count, k) for k in range(count)])


def swapped(block):
    count = lax.axis_size("vocab")
    return lax.ppermute(block, "vocab", [(k, k ^ 1) for k in range(count)])


def tied(value, other):
    return value if other is None else lax.optimization_barrier((value, other))[0]


def ring_ends(block, lead):
    return sent(block, plane_shift(lead, 1)), sent(block, plane_shift(lead, -1))


def ring_far(before, after, lead, gate=None):
    half = before.shape[0] // 2
    low, high = tied(before[:half], gate), tied(after[half:], gate)
    return sent(low, plane_shift(lead, 1)), sent(high, plane_shift(lead, -1))


def block_numbers(core):
    place = lax.axis_index("vocab")
    x, y = place // 2 % side, place // (2 * side)
    lead = jnp.where(core == 0, x, y)
    other = jnp.where(core == 0, y, x)
    leads = (0, -1, 1, 2)
    steps = [(a, 0) for a in leads] + [(a, -1) for a in leads] + [(a, 1) for a in leads]
    steps += [(a, 2) for a in leads]
    ahead = (lead + jnp.array([a for a, _ in steps], jnp.int32)) % side
    across = (other + jnp.array([b for _, b in steps], jnp.int32)) % side
    chip = jnp.where(core == 0, across * side + ahead, ahead * side + across)
    return jnp.append(chip, core).astype(jnp.int32)


def encode(logits, width):
    row = lax.broadcasted_iota(jnp.int32, logits.shape, 0)
    real = row < width
    low = jnp.min(jnp.where(real, logits, -masked_floor), axis=0, keepdims=True)
    high = jnp.max(jnp.where(real, logits, masked_floor), axis=0, keepdims=True)
    base = 0.5 * low + 0.5 * high
    span = jnp.maximum(high - low, 1e-30)
    grade = jnp.ceil(jnp.log2(span / levels) * 256.0)
    inverse = jnp.exp2(grade * (-1.0 / 256.0))
    codes = jnp.clip(jnp.round((logits - base) * inverse), -32767.0, 32767.0)
    size = jnp.ceil(jnp.log2(jnp.maximum(jnp.abs(base), 1e-30) / 32767.0))
    unit = jnp.exp2(size)
    first = jnp.clip(jnp.round(base / unit), -32767.0, 32767.0)
    second = jnp.clip(jnp.round((base - first * unit) / unit * 32767.0), -32767.0, 32767.0)
    for at, value in enumerate((grade, size, first, second)):
        codes = jnp.where(row == width + at, value, codes)
    return codes.astype(jnp.int32).astype(jnp.int16)


def logits_body(numbers, *refs, keep):
    mine, theirs, head, outs = refs[:5], refs[5:10], refs[10], refs[11:-4]
    buffer, weights, total, arrived = refs[-4:]
    width, depth = head.shape[0], mine[0].shape[1]
    count = total.shape[1]
    own_rows = pl.ds(pl.multiple_of(numbers[16] * depth, depth), depth)
    other_rows = pl.ds(pl.multiple_of((1 - numbers[16]) * depth, depth), depth)

    def fetch(at, across, ahead):
        first = mine[across].at[ahead] if across < 3 else mine[3 + ahead // 2].at[ahead % 2]
        second = theirs[ahead].at[across] if ahead < 3 else theirs[3 + across // 2].at[across % 2]
        lanes = pl.ds(pl.multiple_of(numbers[at] * 2 * depth, 2 * depth), 2 * depth)
        return (
            pltpu.make_async_copy(head.at[:, lanes], weights.at[at], arrived.at[at, 0]),
            pltpu.make_async_copy(first, buffer.at[at, own_rows, :], arrived.at[at, 1]),
            pltpu.make_async_copy(second, buffer.at[at, other_rows, :], arrived.at[at, 2]),
        )

    for at in range(16):
        for copy in fetch(at, at // 4, at % 4):
            copy.start()
    total[...] = jnp.zeros(total.shape, jnp.float32)

    def one(at, carry):
        for copy in fetch(at, 0, 0):
            copy.wait()
        total[:width, :] += jnp.dot(weights[at], buffer[at], preferred_element_type=jnp.float32)
        return carry

    lax.fori_loop(0, 16, one, 0)
    for k, out in enumerate(outs):
        logits = total[:, k * 128 : (k + 1) * 128]
        out[...] = logits if k == keep else encode(logits, width)


def group_logits(mine, theirs, head_t, numbers, keep):
    depth, count = mine[0].shape[1:]
    outs = [
        jax.ShapeDtypeStruct((padded, 128), jnp.float32 if k == keep else jnp.int16)
        for k in range(count // 128)
    ]
    return pl.pallas_call(
        functools.partial(logits_body, keep=keep),
        out_shape=outs,
        in_specs=[pl.BlockSpec(memory_space=pltpu.SMEM)] + [pl.BlockSpec(memory_space=pltpu.HBM)] * 11,
        scratch_shapes=[
            pltpu.VMEM((16, 2 * depth, count), jnp.bfloat16),
            pltpu.VMEM((16, head_t.shape[0], 2 * depth), jnp.bfloat16),
            pltpu.VMEM((padded, count), jnp.float32),
            pltpu.SemaphoreType.DMA((16, 3)),
        ],
        compiler_params=pltpu.CompilerParams(vmem_limit_bytes=56 * 2**20),
        cost_estimate=pl.CostEstimate(
            flops=2 * count * head_t.size, transcendentals=0, bytes_accessed=head_t.size * 2
        ),
        name="group_logits",
    )(numbers, *mine, *theirs, head_t)


def order_body(*refs):
    out, width = refs[-1], refs[0].shape[1]
    half = (len(refs) - 1) // 2
    for k, block in enumerate(refs[:-1]):
        out[k // half, :, (k % half) * width : (k % half + 1) * width] = block[...]


def ordered(blocks):
    depth, width = blocks[0].shape
    return pl.pallas_call(
        order_body,
        out_shape=jax.ShapeDtypeStruct((2, depth, len(blocks) // 2 * width), blocks[0].dtype),
        compiler_params=pltpu.CompilerParams(vmem_limit_bytes=vmem_bytes),
        name="ordered",
    )(*blocks)


def line_body(own, before, after, low, high, *outs):
    for k, (out, last) in enumerate(zip(outs, (low, high))):
        out[0] = own[k]
        out[1] = before[k]
        out[2] = after[k]
        out[3] = last[0]


def lines(own, *parts):
    return pl.pallas_call(
        line_body,
        out_shape=[jax.ShapeDtypeStruct((4, *own.shape[1:]), own.dtype)] * 2,
        compiler_params=pltpu.CompilerParams(vmem_limit_bytes=vmem_bytes),
        name="lines",
    )(own, *parts)


def decode_body(place, mask, own, *refs, offsets):
    codes, out, stats, held = refs[:-3], *refs[-3:]
    groups, width, count = held.shape
    here = place[0]
    held[here] = own[:width, :]
    for offset, code in zip(offsets, codes):
        values = code[...].astype(jnp.int32).astype(jnp.float32)
        grade, size = values[width : width + 1], values[width + 1 : width + 2]
        first, second = values[width + 2 : width + 3], values[width + 3 : width + 4]
        base = (first + second * (1.0 / 32767.0)) * jnp.exp2(size)
        step = jnp.exp2(grade * (1.0 / 256.0))
        held[(here - offset) % groups] = values[:width] * step + base
    top = jnp.full((1, count), masked_floor, jnp.float32)
    for k in range(groups):
        span = slice(k * width, (k + 1) * width)
        logits = jnp.where(mask[span, :] > 0.5, held[k], masked_floor)
        out[span, :] = logits
        top = jnp.maximum(top, jnp.max(logits, axis=0, keepdims=True))
    logits = out[...]
    weights = jnp.where(logits > 0.5 * masked_floor, jnp.exp(logits - top), 0.0)
    stats[0:1, :] = top
    stats[1:2, :] = jnp.sum(weights, axis=0, keepdims=True)
    stats[2:3, :] = jnp.sum(weights * logits, axis=0, keepdims=True)


def decoded(mask, own, codes, offsets, width):
    groups = lax.axis_size("rows")
    count = own.shape[1]
    place = lax.axis_index("rows").astype(jnp.int32).reshape(1)
    return pl.pallas_call(
        functools.partial(decode_body, offsets=offsets),
        out_shape=(
            jax.ShapeDtypeStruct((groups * width, count), jnp.float32),
            jax.ShapeDtypeStruct((3, count), jnp.float32),
        ),
        in_specs=[pl.BlockSpec(memory_space=pltpu.SMEM)]
        + [pl.BlockSpec(memory_space=pltpu.VMEM)] * (2 + len(codes)),
        scratch_shapes=[pltpu.VMEM((groups, width, count), jnp.float32)],
        compiler_params=pltpu.CompilerParams(vmem_limit_bytes=vmem_bytes),
        name="decode",
    )(place, mask, own, *codes)


def mask_body(states, table, classes, out):
    entries, count = table.shape[1], states.shape[1]
    chosen = lax.broadcasted_iota(jnp.int32, (entries, count), 0) == states[...]
    chosen = chosen.astype(jnp.float32).astype(jnp.bfloat16)
    words = table[...]
    found = []
    for at in range(4):
        piece = jnp.bitwise_and(jnp.right_shift(words, 8 * at), 255)
        piece = piece.astype(jnp.float32).astype(jnp.bfloat16)
        found.append(jnp.dot(piece, chosen, preferred_element_type=jnp.float32).astype(jnp.int32))
    pieces = jnp.stack(found, axis=1)[:, :, None, :]
    shifts = lax.broadcasted_iota(jnp.int32, (1, 1, 8, 1), 2)
    bits = jnp.bitwise_and(jnp.right_shift(pieces, shifts), 1).reshape(words.shape[0] * 32, count)
    allowed = bits.astype(jnp.float32).astype(jnp.bfloat16)
    total = out.shape[0]
    for at in range(0, total, 128):
        size = min(128, total - at)
        spread = lax.broadcasted_iota(jnp.int32, (allowed.shape[0], 128), 0) == classes[:, at : at + 128]
        spread = spread.astype(jnp.float32).astype(jnp.bfloat16)
        piece = lax.dot_general(
            spread, allowed, (((0,), (0,)), ((), ())), preferred_element_type=jnp.float32
        )
        out[at : at + size, :] = piece[:size]


def token_mask(states, table, class_of):
    total = class_of.shape[0]
    classes = jnp.pad(class_of, (0, -total % 128)).reshape(1, -1)
    return pl.pallas_call(
        mask_body,
        out_shape=jax.ShapeDtypeStruct((total, states.shape[0]), jnp.float32),
        compiler_params=pltpu.CompilerParams(vmem_limit_bytes=vmem_bytes),
        name="mask",
    )(states.reshape(1, -1), table.T, classes)


def merged(shard):
    count = lax.axis_size("vocab")
    copies = jnp.broadcast_to(shard, (count, *shard.shape))
    every = lax.all_to_all(copies, "vocab", split_axis=0, concat_axis=0, tiled=True)
    top = jnp.max(every[:, 0], axis=0)
    scale = jnp.exp(every[:, 0] - top)
    return top, jnp.sum(every[:, 1] * scale, axis=0), jnp.sum(every[:, 2] * scale, axis=0)


def on_device(hidden, head, states, class_of, table):
    count, depth = hidden.shape
    width = head.shape[1]
    core = lax.axis_index("vocab") % 2
    numbers = block_numbers(core)
    hidden_t = hidden.T
    found = [hidden_t if s == 0 else from_row_group(hidden_t, s) for s in (*far_offsets, *near_offsets)]
    block = ordered(found)
    ends = ring_ends(block, True)
    far_line, near_line = lines(block, *ends, *ring_far(*ends, True))

    head_t = head.T
    own_states = lax.dynamic_slice_in_dim(states, lax.axis_index("rows") * count, count, 0)
    mask = token_mask(own_states, table, class_of)

    codes, offsets, own = [], [], None
    behind, made = None, None
    for offset_list, line in ((far_offsets, far_line), (near_offsets, near_line)):
        line = tied(line, behind)
        ends = ring_ends(line, False)
        mine = [line, *ends, *ring_far(*ends, False, made)]
        behind = (mine[3], mine[4])
        theirs = [swapped(part) for part in mine]
        keep = offset_list.index(0) if 0 in offset_list else None
        pieces = group_logits(mine, theirs, head_t, numbers, keep)
        made = pieces[0]
        for s, piece in zip(offset_list, pieces):
            if s == 0:
                own = piece
            else:
                codes.append(from_row_group(piece, -s))
                offsets.append(s)

    logits, stats = decoded(mask, own, codes, tuple(offsets), width)
    peak, total, weighted = merged(stats)
    norm_log = peak + jnp.log(total)
    log_probs = jnp.where(logits > 0.5 * masked_floor, logits - norm_log[None, :], 0.0)
    return log_probs.T, norm_log - weighted / total


def solution(mesh):
    in_specs = (P("rows", "vocab"), P(None, ("vocab", "rows")), P(), P("vocab"), P())
    out_specs = (P("rows", "vocab"), P("rows"))
    return jax.shard_map(
        on_device, mesh=mesh, in_specs=in_specs, out_specs=out_specs, check_vma=False
    )
```

profile of v0, /device:TPU:1, one launch (start us, length us, event | category | flops | bytes accessed | tf_op | source)
XLA Modules:
  0.0 165.6 jit_solution(1743894205673165224)
XLA Ops:
  0.6 1.0 copy.13
  1.6 7.8 %collective-permute-start = (bf16[256,128]{1,0:T(8,128)(2,1)S(1)}, bf16[256,128]{1,0:T(8,128)(2,1)S(1)}, u32[]{:S(2)}, u32[]{:S(2)}) collective-permute-start(bf16[256,128]{1,0:T(8,128)(2,1)S(1)} %bitcast.16), channel_id=1, source_target_pairs={{128,0},{160,32},{192,64},{224,96},{0,128},{32,160},{64,192},{96,2... | collective-permute-start | bytes 196616 | tf_op jit(solution)/shard_map/ppermute | solution.py:37
  9.4 3.3 %collective-permute-start.2 = (bf16[256,128]{1,0:T(8,128)(2,1)S(1)}, bf16[256,128]{1,0:T(8,128)(2,1)S(1)}, u32[]{:S(2)}, u32[]{:S(2)}) collective-permute-start(bf16[256,128]{1,0:T(8,128)(2,1)S(1)} %bitcast.18), channel_id=1, source_target_pairs={{160,0},{192,32},{224,64},{0,96},{32,128},{64,160},{96,192},{128,2... | collective-permute-start | bytes 196616 | tf_op jit(solution)/shard_map/ppermute | solution.py:37
  13.5 1.6 collective-permute-start.4
  15.1 1.9 %collective-permute-start.5 = (bf16[256,128]{1,0:T(8,128)(2,1)S(1)}, bf16[256,128]{1,0:T(8,128)(2,1)S(1)}, u32[]{:S(2)}, u32[]{:S(2)}) collective-permute-start(bf16[256,128]{1,0:T(8,128)(2,1)S(1)} %bitcast.21), channel_id=1, source_target_pairs={{224,0},{0,32},{32,64},{64,96},{96,128},{128,160},{160,192},{192,2... | collective-permute-start | bytes 196616 | tf_op jit(solution)/shard_map/ppermute | solution.py:37
  17.0 2.4 %collective-permute-start.6 = (bf16[256,128]{1,0:T(8,128)(2,1)S(1)}, bf16[256,128]{1,0:T(8,128)(2,1)S(1)}, u32[]{:S(2)}, u32[]{:S(2)}) collective-permute-start(bf16[256,128]{1,0:T(8,128)(2,1)S(1)} %bitcast.22), channel_id=1, source_target_pairs={{32,0},{64,32},{96,64},{128,96},{160,128},{192,160},{224,192},{0,2... | collective-permute-start | bytes 196616 | tf_op jit(solution)/shard_map/ppermute | solution.py:37
  19.4 1.0 collective-permute-done.3.refs_3_
  20.4 1.8 %collective-permute-done.5.refs_5_ = bf16[256,128]{1,0:T(8,128)(2,1)S(1)} collective-permute-done((bf16[256,128]{1,0:T(8,128)(2,1)S(1)}, bf16[256,128]{1,0:T(8,128)(2,1)S(1)}, u32[]{:S(2)}, u32[]{:S(2)}) %collective-permute-start.5) | collective-permute-done | bytes 65568 | tf_op jit(solution)/shard_map/ppermute | solution.py:37
  22.4 2.7 %collective-permute-start.8 = (bf16[2,256,512]{2,1,0:T(8,128)(2,1)S(1)}, bf16[2,256,512]{2,1,0:T(8,128)(2,1)S(1)}, u32[]{:S(2)}, u32[]{:S(2)}) collective-permute-start(bf16[2,256,512]{2,1,0:T(8,128)(2,1)S(1)} %ordered.1.own), channel_id=1, source_target_pairs={{0,6},{1,25},{2,0},{3,27},{4,2},{5,29},{6,4},{7,31},{8,14},{9,1},{... | collective-permute-start | bytes 1572872 | tf_op jit(solution)/shard_map/ppermute | solution.py:32
  25.1 6.1 %collective-permute-done.8.after = bf16[2,256,512]{2,1,0:T(8,128)(2,1)S(1)} collective-permute-done((bf16[2,256,512]{2,1,0:T(8,128)(2,1)S(1)}, bf16[2,256,512]{2,1,0:T(8,128)(2,1)S(1)}, u32[]{:S(2)}, u32[]{:S(2)}) %collective-permute-start.8) | collective-permute-done | bytes 524320 | tf_op jit(solution)/shard_map/ppermute | solution.py:32
  31.2 3.5 %collective-permute-start.10 = (bf16[1,256,512]{2,1,0:T(8,128)(2,1)S(1)}, bf16[1,256,512]{2,1,0:T(8,128)(2,1)S(1)}, u32[]{:S(2)}, u32[]{:S(2)}) collective-permute-start(bf16[1,256,512]{2,1,0:T(8,128)(2,1)S(1)} %slice.38), channel_id=1, source_target_pairs={{0,6},{1,25},{2,0},{3,27},{4,2},{5,29},{6,4},{7,31},{8,14},{9,1},{... | collective-permute-start | bytes 786440 | tf_op jit(solution)/shard_map/ppermute | solution.py:32
  34.8 3.2 %collective-permute-done.10.high = bf16[1,256,512]{2,1,0:T(8,128)(2,1)S(1)} collective-permute-done((bf16[1,256,512]{2,1,0:T(8,128)(2,1)S(1)}, bf16[1,256,512]{2,1,0:T(8,128)(2,1)S(1)}, u32[]{:S(2)}, u32[]{:S(2)}) %collective-permute-start.10) | collective-permute-done | bytes 262176 | tf_op jit(solution)/shard_map/ppermute | solution.py:32
  38.0 3.2 %collective-permute-done.9.low = bf16[1,256,512]{2,1,0:T(8,128)(2,1)S(1)} collective-permute-done((bf16[1,256,512]{2,1,0:T(8,128)(2,1)S(1)}, bf16[1,256,512]{2,1,0:T(8,128)(2,1)S(1)}, u32[]{:S(2)}, u32[]{:S(2)}) %collective-permute-start.9) | collective-permute-done | bytes 262176 | tf_op jit(solution)/shard_map/ppermute | solution.py:32
  41.4 1.0 collective-permute-start.11
  42.4 1.9 %collective-permute-start.13 = (bf16[4,256,512]{2,1,0:T(8,128)(2,1)S(1)}, bf16[4,256,512]{2,1,0:T(8,128)(2,1)}, u32[]{:S(2)}, u32[]{:S(2)}) collective-permute-start(bf16[4,256,512]{2,1,0:T(8,128)(2,1)S(1)} %get-tuple-element.18.refs_0_), channel_id=1, source_target_pairs={{0,24},{1,7},{2,26},{3,1},{4,28},{5,3},{6,30},{7,5},{8,0},{9,15},{... | collective-permute-start | bytes 3145736 | tf_op jit(solution)/shard_map/ppermute | solution.py:32
  44.4 6.0 %collective-permute-start.17 = (bf16[4,256,512]{2,1,0:T(8,128)(2,1)S(1)}, bf16[4,256,512]{2,1,0:T(8,128)(2,1)S(1)}, u32[]{:S(2)}, u32[]{:S(2)}) collective-permute-start(bf16[4,256,512]{2,1,0:T(8,128)(2,1)S(1)} %get-tuple-element.18.refs_0_), channel_id=1, source_target_pairs={{0,1},{1,0},{2,3},{3,2},{4,5},{5,4},{6,7},{7,6},{8,9},{9,8},{10,11... | collective-permute-start | bytes 3145736 | tf_op jit(solution)/shard_map/ppermute | solution.py:42
  50.4 6.4 %collective-permute-done.11.refs_1_ = bf16[4,256,512]{2,1,0:T(8,128)(2,1)S(1)} collective-permute-done((bf16[4,256,512]{2,1,0:T(8,128)(2,1)S(1)}, bf16[4,256,512]{2,1,0:T(8,128)(2,1)S(1)}, u32[]{:S(2)}, u32[]{:S(2)}) %collective-permute-start.11) | collective-permute-done | bytes 1048608 | tf_op jit(solution)/shard_map/ppermute | solution.py:32
  56.9 1.3 slice.40
  58.2 2.7 %collective-permute-start.14 = (bf16[2,256,512]{2,1,0:T(8,128)(2,1)S(1)}, bf16[2,256,512]{2,1,0:T(8,128)(2,1)}, u32[]{:S(2)}, u32[]{:S(2)}) collective-permute-start(bf16[2,256,512]{2,1,0:T(8,128)(2,1)S(1)} %slice.40), channel_id=1, source_target_pairs={{0,24},{1,7},{2,26},{3,1},{4,28},{5,3},{6,30},{7,5},{8,0},{9,15},{... | collective-permute-start | bytes 1572872 | tf_op jit(solution)/shard_map/ppermute | solution.py:32
  60.9 5.2 %collective-permute-done.12.refs_3_ = bf16[2,256,512]{2,1,0:T(8,128)(2,1)S(1)} collective-permute-done((bf16[2,256,512]{2,1,0:T(8,128)(2,1)S(1)}, bf16[2,256,512]{2,1,0:T(8,128)(2,1)S(1)}, u32[]{:S(2)}, u32[]{:S(2)}) %collective-permute-start.12) | collective-permute-done | bytes 524320 | tf_op jit(solution)/shard_map/ppermute | solution.py:32
  66.1 7.5 %collective-permute-start.20 = (bf16[2,256,512]{2,1,0:T(8,128)(2,1)S(1)}, bf16[2,256,512]{2,1,0:T(8,128)(2,1)S(1)}, u32[]{:S(2)}, u32[]{:S(2)}) collective-permute-start(bf16[2,256,512]{2,1,0:T(8,128)(2,1)S(1)} %collective-permute-done.12.refs_3_), channel_id=1, source_target_pairs={{0,1},{1,0},{2,3},{3,2},{4,5},{5,4},{6,7},{7,6},{8,9},{9,8},{10,11... | collective-permute-start | bytes 1572872 | tf_op jit(solution)/shard_map/ppermute | solution.py:42
  74.1 1.0 copy-done.13
  75.1 1.5 collective-permute-start.15
  77.4 2.8 %collective-permute-start.21 = (bf16[2,256,512]{2,1,0:T(8,128)(2,1)}, bf16[2,256,512]{2,1,0:T(8,128)(2,1)}, u32[]{:S(2)}, u32[]{:S(2)}) collective-permute-start(bf16[2,256,512]{2,1,0:T(8,128)(2,1)} %collective-permute-done.14.refs_4_), channel_id=1, source_target_pairs={{0,1},{1,0},{2,3},{3,2},{4,5},{5,4},{6,7},{7,6},{8,9},{9,8},{10,11... | collective-permute-start | bytes 1572872 | tf_op jit(solution)/shard_map/ppermute | solution.py:42
  80.9 1.2 collective-permute-done.21.refs_9_
  82.5 11.3 %group_logits.2 = (s16[608,128]{1,0:T(8,128)(2,1)}, s16[608,128]{1,0:T(8,128)(2,1)}, s16[608,128]{1,0:T(8,128)(2,1)}, s16[608,128]{1,0:T(8,128)(2,1)}) custom-call(s32[17]{0:T(128)} %pad_add_fusion.numbers, bf16[4,256,512]{2,1,0:T(8,128)(2,1)} %copy-done.8, bf16[4,256,512]{2,1,0:T(8,128)(2,1)} %copy-done.9, ...), custom_call_target="tpu_custom_call" | custom-call | flops 4982833152 | bytes 9732096 | tf_op jit(solution)/shard_map/group_logits/pallas_call | solution.py:133
  93.8 1.1 slice.42
  95.0 1.1 slice.41
  96.1 1.5 collective-permute-start.22
  97.6 2.0 %collective-permute-start.25 = (bf16[4,256,512]{2,1,0:T(8,128)(2,1)}, bf16[4,256,512]{2,1,0:T(8,128)(2,1)S(1)}, u32[]{:S(2)}, u32[]{:S(2)}) collective-permute-start(bf16[4,256,512]{2,1,0:T(8,128)(2,1)} %collective-permute-done.15.refs_1_), channel_id=1, source_target_pairs={{0,1},{1,0},{2,3},{3,2},{4,5},{5,4},{6,7},{7,6},{8,9},{9,8},{10,11... | collective-permute-start | bytes 3145736 | tf_op jit(solution)/shard_map/ppermute | solution.py:42
  99.7 3.6 %collective-permute-done.23.refs_4_ = bf16[2,256,512]{2,1,0:T(8,128)(2,1)S(1)} collective-permute-done((bf16[2,256,512]{2,1,0:T(8,128)(2,1)S(1)}, bf16[2,256,512]{2,1,0:T(8,128)(2,1)S(1)}, u32[]{:S(2)}, u32[]{:S(2)}) %collective-permute-start.23) | collective-permute-done | bytes 524320 | tf_op jit(solution)/shard_map/ppermute | solution.py:32
  103.3 1.7 %collective-permute-start.28 = (bf16[2,256,512]{2,1,0:T(8,128)(2,1)S(1)}, bf16[2,256,512]{2,1,0:T(8,128)(2,1)S(1)}, u32[]{:S(2)}, u32[]{:S(2)}) collective-permute-start(bf16[2,256,512]{2,1,0:T(8,128)(2,1)S(1)} %collective-permute-done.23.refs_4_), channel_id=1, source_target_pairs={{0,1},{1,0},{2,3},{3,2},{4,5},{5,4},{6,7},{7,6},{8,9},{9,8},{10,11... | collective-permute-start | bytes 1572872 | tf_op jit(solution)/shard_map/ppermute | solution.py:42
  105.7 4.2 %collective-permute-start.27 = (bf16[2,256,512]{2,1,0:T(8,128)(2,1)S(1)}, bf16[2,256,512]{2,1,0:T(8,128)(2,1)S(1)}, u32[]{:S(2)}, u32[]{:S(2)}) collective-permute-start(bf16[2,256,512]{2,1,0:T(8,128)(2,1)S(1)} %collective-permute-done.22.refs_3_), channel_id=1, source_target_pairs={{0,1},{1,0},{2,3},{3,2},{4,5},{5,4},{6,7},{7,6},{8,9},{9,8},{10,11... | collective-permute-start | bytes 1572872 | tf_op jit(solution)/shard_map/ppermute | solution.py:42
  109.9 6.2 %collective-permute-start.29 = (s16[608,128]{1,0:T(8,128)(2,1)}, s16[608,128]{1,0:T(8,128)(2,1)S(1)}, u32[]{:S(2)}, u32[]{:S(2)}) collective-permute-start(s16[608,128]{1,0:T(8,128)(2,1)} %get-tuple-element.20), channel_id=1, source_target_pairs={{128,0},{160,32},{192,64},{224,96},{0,128},{32,160},{64,192},{96,2... | collective-permute-start | bytes 466952 | tf_op jit(solution)/shard_map/ppermute | solution.py:37
  116.1 4.5 %collective-permute-start.31 = (s16[608,128]{1,0:T(8,128)(2,1)}, s16[608,128]{1,0:T(8,128)(2,1)S(1)}, u32[]{:S(2)}, u32[]{:S(2)}) collective-permute-start(s16[608,128]{1,0:T(8,128)(2,1)} %get-tuple-element.25), channel_id=1, source_target_pairs={{96,0},{128,32},{160,64},{192,96},{224,128},{0,160},{32,192},{64,2... | collective-permute-start | bytes 466952 | tf_op jit(solution)/shard_map/ppermute | solution.py:37
  120.6 1.4 collective-permute-start.32
  122.1 1.0 copy-done.16
  123.1 11.4 %group_logits.3 = (s16[608,128]{1,0:T(8,128)(2,1)}, s16[608,128]{1,0:T(8,128)(2,1)}, s16[608,128]{1,0:T(8,128)(2,1)}, f32[608,128]{1,0:T(8,128)}) custom-call(s32[17]{0:T(128)} %pad_add_fusion.numbers, bf16[4,256,512]{2,1,0:T(8,128)(2,1)} %copy-done.7, bf16[4,256,512]{2,1,0:T(8,128)(2,1)} %collective-permute-done.15.refs_1_, ...), custom_call_target="tpu_custom_call" | custom-call | flops 4982833152 | bytes 9732096 | tf_op jit(solution)/shard_map/group_logits/pallas_call | solution.py:133
  134.4 2.5 %collective-permute-start.33 = (s16[608,128]{1,0:T(8,128)(2,1)}, s16[608,128]{1,0:T(8,128)(2,1)S(1)}, u32[]{:S(2)}, u32[]{:S(2)}) collective-permute-start(s16[608,128]{1,0:T(8,128)(2,1)} %get-tuple-element.27), channel_id=1, source_target_pairs={{64,0},{96,32},{128,64},{160,96},{192,128},{224,160},{0,192},{32,2... | collective-permute-start | bytes 466952 | tf_op jit(solution)/shard_map/ppermute | solution.py:37
  137.0 1.5 collective-permute-start.35
  138.6 1.3 mask.1
  139.9 3.8 %collective-permute-done.33.refs_4_ = s16[608,128]{1,0:T(8,128)(2,1)S(1)} collective-permute-done((s16[608,128]{1,0:T(8,128)(2,1)}, s16[608,128]{1,0:T(8,128)(2,1)S(1)}, u32[]{:S(2)}, u32[]{:S(2)}) %collective-permute-start.33) | collective-permute-done | bytes 155680 | tf_op jit(solution)/shard_map/ppermute | solution.py:37
  143.7 3.0 %collective-permute-done.34.refs_5_ = s16[608,128]{1,0:T(8,128)(2,1)S(1)} collective-permute-done((s16[608,128]{1,0:T(8,128)(2,1)}, s16[608,128]{1,0:T(8,128)(2,1)S(1)}, u32[]{:S(2)}, u32[]{:S(2)}) %collective-permute-start.34) | collective-permute-done | bytes 155680 | tf_op jit(solution)/shard_map/ppermute | solution.py:37
  148.0 0.9 copy-done.3
  148.9 0.9 copy-done.5
  149.8 1.6 decode.1
  151.4 12.0 %all_to_all.5 = f32[32,3,128]{2,1,0:T(4,128)S(1)} all-to-all(f32[32,3,128]{2,1,0:T(4,128)S(1)} %broadcast_in_dim.9), channel_id=1, replica_groups=mesh['rows'=8,'vocab'=32] {'vocab'}, dimensions={0} | all-to-all | bytes 98304 | tf_op jit(solution)/shard_map/all_to_all | solution.py:267
  163.9 1.7 %select_bitcast_fusion = f32[128,4752]{0,1:T(8,128)} fusion(f32[4752,128]{1,0:T(8,128)S(1)} %get-tuple-element.30, f32[128]{0:T(128)S(1)} %get-tuple-element.38), kind=kLoop, calls=%fused_computation | loop fusion | flops 1824768 | bytes 4866560 | tf_op jit(solution)/shard_map/transpose | solution.py:310
  (95 shorter events, 6.7 us)
Async XLA Ops:
  0.6 137.8 %copy-start = (s32[1024]{0:T(1024)S(1)}, s32[1024]{0:T(1024)}, u32[]{:S(2)}) copy-start(s32[1024]{0:T(1024)} %param.9) | copy-start | bytes 12292
  1.6 13.5 %collective-permute-start = (bf16[256,128]{1,0:T(8,128)(2,1)S(1)}, bf16[256,128]{1,0:T(8,128)(2,1)S(1)}, u32[]{:S(2)}, u32[]{:S(2)}) collective-permute-start(bf16[256,128]{1,0:T(8,128)(2,1)S(1)} %bitcast.16), channel_id=1, source_target_pairs={{128,0},{160,32},{192,64},{224,96},{0,128},{32,160},{64,192},{96,2... | collective-permute-start | bytes 196616 | tf_op jit(solution)/shard_map/ppermute | solution.py:37
  9.4 7.6 %collective-permute-start.1 = (bf16[256,128]{1,0:T(8,128)(2,1)S(1)}, bf16[256,128]{1,0:T(8,128)(2,1)S(1)}, u32[]{:S(2)}, u32[]{:S(2)}) collective-permute-start(bf16[256,128]{1,0:T(8,128)(2,1)S(1)} %bitcast.17), channel_id=1, source_target_pairs={{96,0},{128,32},{160,64},{192,96},{224,128},{0,160},{32,192},{64,2... | collective-permute-start | bytes 196616 | tf_op jit(solution)/shard_map/ppermute | solution.py:37
  9.4 10.0 %collective-permute-start.2 = (bf16[256,128]{1,0:T(8,128)(2,1)S(1)}, bf16[256,128]{1,0:T(8,128)(2,1)S(1)}, u32[]{:S(2)}, u32[]{:S(2)}) collective-permute-start(bf16[256,128]{1,0:T(8,128)(2,1)S(1)} %bitcast.18), channel_id=1, source_target_pairs={{160,0},{192,32},{224,64},{0,96},{32,128},{64,160},{96,192},{128,2... | collective-permute-start | bytes 196616 | tf_op jit(solution)/shard_map/ppermute | solution.py:37
  12.7 7.7 %collective-permute-start.3 = (bf16[256,128]{1,0:T(8,128)(2,1)S(1)}, bf16[256,128]{1,0:T(8,128)(2,1)S(1)}, u32[]{:S(2)}, u32[]{:S(2)}) collective-permute-start(bf16[256,128]{1,0:T(8,128)(2,1)S(1)} %bitcast.19), channel_id=1, source_target_pairs={{64,0},{96,32},{128,64},{160,96},{192,128},{224,160},{0,192},{32,2... | collective-permute-start | bytes 196616 | tf_op jit(solution)/shard_map/ppermute | solution.py:37
  13.5 7.0 %collective-permute-start.4 = (bf16[256,128]{1,0:T(8,128)(2,1)S(1)}, bf16[256,128]{1,0:T(8,128)(2,1)S(1)}, u32[]{:S(2)}, u32[]{:S(2)}) collective-permute-start(bf16[256,128]{1,0:T(8,128)(2,1)S(1)} %bitcast.20), channel_id=1, source_target_pairs={{192,0},{224,32},{0,64},{32,96},{64,128},{96,160},{128,192},{160,2... | collective-permute-start | bytes 196616 | tf_op jit(solution)/shard_map/ppermute | solution.py:37
  15.1 7.2 %collective-permute-start.5 = (bf16[256,128]{1,0:T(8,128)(2,1)S(1)}, bf16[256,128]{1,0:T(8,128)(2,1)S(1)}, u32[]{:S(2)}, u32[]{:S(2)}) collective-permute-start(bf16[256,128]{1,0:T(8,128)(2,1)S(1)} %bitcast.21), channel_id=1, source_target_pairs={{224,0},{0,32},{32,64},{64,96},{96,128},{128,160},{160,192},{192,2... | collective-permute-start | bytes 196616 | tf_op jit(solution)/shard_map/ppermute | solution.py:37
  17.0 5.3 %collective-permute-start.6 = (bf16[256,128]{1,0:T(8,128)(2,1)S(1)}, bf16[256,128]{1,0:T(8,128)(2,1)S(1)}, u32[]{:S(2)}, u32[]{:S(2)}) collective-permute-start(bf16[256,128]{1,0:T(8,128)(2,1)S(1)} %bitcast.22), channel_id=1, source_target_pairs={{32,0},{64,32},{96,64},{128,96},{160,128},{192,160},{224,192},{0,2... | collective-permute-start | bytes 196616 | tf_op jit(solution)/shard_map/ppermute | solution.py:37
  22.4 8.8 %collective-permute-start.8 = (bf16[2,256,512]{2,1,0:T(8,128)(2,1)S(1)}, bf16[2,256,512]{2,1,0:T(8,128)(2,1)S(1)}, u32[]{:S(2)}, u32[]{:S(2)}) collective-permute-start(bf16[2,256,512]{2,1,0:T(8,128)(2,1)S(1)} %ordered.1.own), channel_id=1, source_target_pairs={{0,6},{1,25},{2,0},{3,27},{4,2},{5,29},{6,4},{7,31},{8,14},{9,1},{... | collective-permute-start | bytes 1572872 | tf_op jit(solution)/shard_map/ppermute | solution.py:32
  25.0 9.7 %collective-permute-start.7 = (bf16[2,256,512]{2,1,0:T(8,128)(2,1)S(1)}, bf16[2,256,512]{2,1,0:T(8,128)(2,1)S(1)}, u32[]{:S(2)}, u32[]{:S(2)}) collective-permute-start(bf16[2,256,512]{2,1,0:T(8,128)(2,1)S(1)} %ordered.1.own), channel_id=1, source_target_pairs={{0,2},{1,9},{2,4},{3,11},{4,6},{5,13},{6,0},{7,15},{8,10},{9,17},{... | collective-permute-start | bytes 1572872 | tf_op jit(solution)/shard_map/ppermute | solution.py:32
  31.2 49.0 %copy-start.11 = (s32[16]{0:T(128)S(1)}, s32[16]{0:T(128)}, u32[]{:S(2)}) copy-start(s32[16]{0:T(128)} %constant.82.clone) | copy-start | bytes 196
  31.2 49.0 %copy-start.12 = (s32[16]{0:T(128)S(1)}, s32[16]{0:T(128)}, u32[]{:S(2)}) copy-start(s32[16]{0:T(128)} %constant.83.clone) | copy-start | bytes 196
  31.2 6.8 %collective-permute-start.10 = (bf16[1,256,512]{2,1,0:T(8,128)(2,1)S(1)}, bf16[1,256,512]{2,1,0:T(8,128)(2,1)S(1)}, u32[]{:S(2)}, u32[]{:S(2)}) collective-permute-start(bf16[1,256,512]{2,1,0:T(8,128)(2,1)S(1)} %slice.38), channel_id=1, source_target_pairs={{0,6},{1,25},{2,0},{3,27},{4,2},{5,29},{6,4},{7,31},{8,14},{9,1},{... | collective-permute-start | bytes 786440 | tf_op jit(solution)/shard_map/ppermute | solution.py:32
  34.7 6.5 %collective-permute-start.9 = (bf16[1,256,512]{2,1,0:T(8,128)(2,1)S(1)}, bf16[1,256,512]{2,1,0:T(8,128)(2,1)S(1)}, u32[]{:S(2)}, u32[]{:S(2)}) collective-permute-start(bf16[1,256,512]{2,1,0:T(8,128)(2,1)S(1)} %slice.37), channel_id=1, source_target_pairs={{0,2},{1,9},{2,4},{3,11},{4,6},{5,13},{6,0},{7,15},{8,10},{9,17},{... | collective-permute-start | bytes 786440 | tf_op jit(solution)/shard_map/ppermute | solution.py:32
  41.4 41.1 %copy-start.8 = (bf16[4,256,512]{2,1,0:T(8,128)(2,1)}, bf16[4,256,512]{2,1,0:T(8,128)(2,1)S(1)}, u32[]{:S(2)}) copy-start(bf16[4,256,512]{2,1,0:T(8,128)(2,1)S(1)} %get-tuple-element.18.refs_0_) | copy-start | bytes 3145732
  41.4 52.4 %copy-start.7 = (bf16[4,256,512]{2,1,0:T(8,128)(2,1)}, bf16[4,256,512]{2,1,0:T(8,128)(2,1)S(1)}, u32[]{:S(2)}) copy-start(bf16[4,256,512]{2,1,0:T(8,128)(2,1)S(1)} %get-tuple-element.19.refs_0_) | copy-start | bytes 3145732
  41.4 15.3 %collective-permute-start.11 = (bf16[4,256,512]{2,1,0:T(8,128)(2,1)S(1)}, bf16[4,256,512]{2,1,0:T(8,128)(2,1)S(1)}, u32[]{:S(2)}, u32[]{:S(2)}) collective-permute-start(bf16[4,256,512]{2,1,0:T(8,128)(2,1)S(1)} %get-tuple-element.18.refs_0_), channel_id=1, source_target_pairs={{0,8},{1,3},{2,10},{3,5},{4,12},{5,7},{6,14},{7,1},{8,16},{9,11},{... | collective-permute-start | bytes 3145736 | tf_op jit(solution)/shard_map/ppermute | solution.py:32
  42.4 14.5 %collective-permute-start.13 = (bf16[4,256,512]{2,1,0:T(8,128)(2,1)S(1)}, bf16[4,256,512]{2,1,0:T(8,128)(2,1)}, u32[]{:S(2)}, u32[]{:S(2)}) collective-permute-start(bf16[4,256,512]{2,1,0:T(8,128)(2,1)S(1)} %get-tuple-element.18.refs_0_), channel_id=1, source_target_pairs={{0,24},{1,7},{2,26},{3,1},{4,28},{5,3},{6,30},{7,5},{8,0},{9,15},{... | collective-permute-start | bytes 3145736 | tf_op jit(solution)/shard_map/ppermute | solution.py:32
  44.4 29.7 %collective-permute-start.17 = (bf16[4,256,512]{2,1,0:T(8,128)(2,1)S(1)}, bf16[4,256,512]{2,1,0:T(8,128)(2,1)S(1)}, u32[]{:S(2)}, u32[]{:S(2)}) collective-permute-start(bf16[4,256,512]{2,1,0:T(8,128)(2,1)S(1)} %get-tuple-element.18.refs_0_), channel_id=1, source_target_pairs={{0,1},{1,0},{2,3},{3,2},{4,5},{5,4},{6,7},{7,6},{8,9},{9,8},{10,11... | collective-permute-start | bytes 3145736 | tf_op jit(solution)/shard_map/ppermute | solution.py:42
  56.7 25.7 %copy-start.9 = (bf16[4,256,512]{2,1,0:T(8,128)(2,1)}, bf16[4,256,512]{2,1,0:T(8,128)(2,1)S(1)}, u32[]{:S(2)}) copy-start(bf16[4,256,512]{2,1,0:T(8,128)(2,1)S(1)} %collective-permute-done.11.refs_1_) | copy-start | bytes 3145732
  56.8 9.3 %collective-permute-start.12 = (bf16[2,256,512]{2,1,0:T(8,128)(2,1)S(1)}, bf16[2,256,512]{2,1,0:T(8,128)(2,1)S(1)}, u32[]{:S(2)}, u32[]{:S(2)}) collective-permute-start(bf16[2,256,512]{2,1,0:T(8,128)(2,1)S(1)} %slice.39), channel_id=1, source_target_pairs={{0,8},{1,3},{2,10},{3,5},{4,12},{5,7},{6,14},{7,1},{8,16},{9,11},{... | collective-permute-start | bytes 1572872 | tf_op jit(solution)/shard_map/ppermute | solution.py:32
  58.2 15.9 %collective-permute-start.14 = (bf16[2,256,512]{2,1,0:T(8,128)(2,1)S(1)}, bf16[2,256,512]{2,1,0:T(8,128)(2,1)}, u32[]{:S(2)}, u32[]{:S(2)}) collective-permute-start(bf16[2,256,512]{2,1,0:T(8,128)(2,1)S(1)} %slice.40), channel_id=1, source_target_pairs={{0,24},{1,7},{2,26},{3,1},{4,28},{5,3},{6,30},{7,5},{8,0},{9,15},{... | collective-permute-start | bytes 1572872 | tf_op jit(solution)/shard_map/ppermute | solution.py:32
  66.1 10.5 %collective-permute-start.20 = (bf16[2,256,512]{2,1,0:T(8,128)(2,1)S(1)}, bf16[2,256,512]{2,1,0:T(8,128)(2,1)S(1)}, u32[]{:S(2)}, u32[]{:S(2)}) collective-permute-start(bf16[2,256,512]{2,1,0:T(8,128)(2,1)S(1)} %collective-permute-done.12.refs_3_), channel_id=1, source_target_pairs={{0,1},{1,0},{2,3},{3,2},{4,5},{5,4},{6,7},{7,6},{8,9},{9,8},{10,11... | collective-permute-start | bytes 1572872 | tf_op jit(solution)/shard_map/ppermute | solution.py:42
  73.6 8.9 %collective-permute-start.18 = (bf16[4,256,512]{2,1,0:T(8,128)(2,1)S(1)}, bf16[4,256,512]{2,1,0:T(8,128)(2,1)}, u32[]{:S(2)}, u32[]{:S(2)}) collective-permute-start(bf16[4,256,512]{2,1,0:T(8,128)(2,1)S(1)} %collective-permute-done.11.refs_1_), channel_id=1, source_target_pairs={{0,1},{1,0},{2,3},{3,2},{4,5},{5,4},{6,7},{7,6},{8,9},{9,8},{10,11... | collective-permute-start | bytes 3145736 | tf_op jit(solution)/shard_map/ppermute | solution.py:42
  73.6 8.9 %collective-permute-start.19 = (bf16[4,256,512]{2,1,0:T(8,128)(2,1)}, bf16[4,256,512]{2,1,0:T(8,128)(2,1)}, u32[]{:S(2)}, u32[]{:S(2)}) collective-permute-start(bf16[4,256,512]{2,1,0:T(8,128)(2,1)} %collective-permute-done.13.refs_2_), channel_id=1, source_target_pairs={{0,1},{1,0},{2,3},{3,2},{4,5},{5,4},{6,7},{7,6},{8,9},{9,8},{10,11... | collective-permute-start | bytes 3145736 | tf_op jit(solution)/shard_map/ppermute | solution.py:42
  74.1 19.7 %collective-permute-start.16 = (bf16[4,256,512]{2,1,0:T(8,128)(2,1)S(1)}, bf16[4,256,512]{2,1,0:T(8,128)(2,1)}, u32[]{:S(2)}, u32[]{:S(2)}) collective-permute-start(bf16[4,256,512]{2,1,0:T(8,128)(2,1)S(1)} %get-tuple-element.19.refs_0_), channel_id=1, source_target_pairs={{0,24},{1,7},{2,26},{3,1},{4,28},{5,3},{6,30},{7,5},{8,0},{9,15},{... | collective-permute-start | bytes 3145736 | tf_op jit(solution)/shard_map/ppermute | solution.py:32
  75.1 19.8 %collective-permute-start.15 = (bf16[4,256,512]{2,1,0:T(8,128)(2,1)S(1)}, bf16[4,256,512]{2,1,0:T(8,128)(2,1)}, u32[]{:S(2)}, u32[]{:S(2)}) collective-permute-start(bf16[4,256,512]{2,1,0:T(8,128)(2,1)S(1)} %get-tuple-element.19.refs_0_), channel_id=1, source_target_pairs={{0,8},{1,3},{2,10},{3,5},{4,12},{5,7},{6,14},{7,1},{8,16},{9,11},{... | collective-permute-start | bytes 3145736 | tf_op jit(solution)/shard_map/ppermute | solution.py:32
  77.4 4.7 %collective-permute-start.21 = (bf16[2,256,512]{2,1,0:T(8,128)(2,1)}, bf16[2,256,512]{2,1,0:T(8,128)(2,1)}, u32[]{:S(2)}, u32[]{:S(2)}) collective-permute-start(bf16[2,256,512]{2,1,0:T(8,128)(2,1)} %collective-permute-done.14.refs_4_), channel_id=1, source_target_pairs={{0,1},{1,0},{2,3},{3,2},{4,5},{5,4},{6,7},{7,6},{8,9},{9,8},{10,11... | collective-permute-start | bytes 1572872 | tf_op jit(solution)/shard_map/ppermute | solution.py:42
  82.1 27.8 %collective-permute-start.24 = (bf16[4,256,512]{2,1,0:T(8,128)(2,1)S(1)}, bf16[4,256,512]{2,1,0:T(8,128)(2,1)S(1)}, u32[]{:S(2)}, u32[]{:S(2)}) collective-permute-start(bf16[4,256,512]{2,1,0:T(8,128)(2,1)S(1)} %get-tuple-element.19.refs_0_), channel_id=1, source_target_pairs={{0,1},{1,0},{2,3},{3,2},{4,5},{5,4},{6,7},{7,6},{8,9},{9,8},{10,11... | collective-permute-start | bytes 3145736 | tf_op jit(solution)/shard_map/ppermute | solution.py:42
  94.9 8.4 %collective-permute-start.23 = (bf16[2,256,512]{2,1,0:T(8,128)(2,1)S(1)}, bf16[2,256,512]{2,1,0:T(8,128)(2,1)S(1)}, u32[]{:S(2)}, u32[]{:S(2)}) collective-permute-start(bf16[2,256,512]{2,1,0:T(8,128)(2,1)S(1)} %slice.42), channel_id=1, source_target_pairs={{0,24},{1,7},{2,26},{3,1},{4,28},{5,3},{6,30},{7,5},{8,0},{9,15},{... | collective-permute-start | bytes 1572872 | tf_op jit(solution)/shard_map/ppermute | solution.py:32
  96.1 9.6 %collective-permute-start.22 = (bf16[2,256,512]{2,1,0:T(8,128)(2,1)S(1)}, bf16[2,256,512]{2,1,0:T(8,128)(2,1)S(1)}, u32[]{:S(2)}, u32[]{:S(2)}) collective-permute-start(bf16[2,256,512]{2,1,0:T(8,128)(2,1)S(1)} %slice.41), channel_id=1, source_target_pairs={{0,8},{1,3},{2,10},{3,5},{4,12},{5,7},{6,14},{7,1},{8,16},{9,11},{... | collective-permute-start | bytes 1572872 | tf_op jit(solution)/shard_map/ppermute | solution.py:32
  97.6 23.0 %collective-permute-start.25 = (bf16[4,256,512]{2,1,0:T(8,128)(2,1)}, bf16[4,256,512]{2,1,0:T(8,128)(2,1)S(1)}, u32[]{:S(2)}, u32[]{:S(2)}) collective-permute-start(bf16[4,256,512]{2,1,0:T(8,128)(2,1)} %collective-permute-done.15.refs_1_), channel_id=1, source_target_pairs={{0,1},{1,0},{2,3},{3,2},{4,5},{5,4},{6,7},{7,6},{8,9},{9,8},{10,11... | collective-permute-start | bytes 3145736 | tf_op jit(solution)/shard_map/ppermute | solution.py:42
  99.6 22.4 %collective-permute-start.26 = (bf16[4,256,512]{2,1,0:T(8,128)(2,1)}, bf16[4,256,512]{2,1,0:T(8,128)(2,1)S(1)}, u32[]{:S(2)}, u32[]{:S(2)}) collective-permute-start(bf16[4,256,512]{2,1,0:T(8,128)(2,1)} %collective-permute-done.16.refs_2_), channel_id=1, source_target_pairs={{0,1},{1,0},{2,3},{3,2},{4,5},{5,4},{6,7},{7,6},{8,9},{9,8},{10,11... | collective-permute-start | bytes 3145736 | tf_op jit(solution)/shard_map/ppermute | solution.py:42
  103.3 18.7 %copy-start.19 = (bf16[2,256,512]{2,1,0:T(8,128)(2,1)}, bf16[2,256,512]{2,1,0:T(8,128)(2,1)S(1)}, u32[]{:S(2)}) copy-start(bf16[2,256,512]{2,1,0:T(8,128)(2,1)S(1)} %collective-permute-done.23.refs_4_) | copy-start | bytes 1572868
  103.3 12.8 %collective-permute-start.28 = (bf16[2,256,512]{2,1,0:T(8,128)(2,1)S(1)}, bf16[2,256,512]{2,1,0:T(8,128)(2,1)S(1)}, u32[]{:S(2)}, u32[]{:S(2)}) collective-permute-start(bf16[2,256,512]{2,1,0:T(8,128)(2,1)S(1)} %collective-permute-done.23.refs_4_), channel_id=1, source_target_pairs={{0,1},{1,0},{2,3},{3,2},{4,5},{5,4},{6,7},{7,6},{8,9},{9,8},{10,11... | collective-permute-start | bytes 1572872 | tf_op jit(solution)/shard_map/ppermute | solution.py:42
  105.7 16.3 %copy-start.20 = (bf16[2,256,512]{2,1,0:T(8,128)(2,1)}, bf16[2,256,512]{2,1,0:T(8,128)(2,1)S(1)}, u32[]{:S(2)}) copy-start(bf16[2,256,512]{2,1,0:T(8,128)(2,1)S(1)} %collective-permute-done.22.refs_3_) | copy-start | bytes 1572868
  105.7 10.4 %collective-permute-start.27 = (bf16[2,256,512]{2,1,0:T(8,128)(2,1)S(1)}, bf16[2,256,512]{2,1,0:T(8,128)(2,1)S(1)}, u32[]{:S(2)}, u32[]{:S(2)}) collective-permute-start(bf16[2,256,512]{2,1,0:T(8,128)(2,1)S(1)} %collective-permute-done.22.refs_3_), channel_id=1, source_target_pairs={{0,1},{1,0},{2,3},{3,2},{4,5},{5,4},{6,7},{7,6},{8,9},{9,8},{10,11... | collective-permute-start | bytes 1572872 | tf_op jit(solution)/shard_map/ppermute | solution.py:42
  109.9 12.1 %copy-start.14 = (bf16[4,256,512]{2,1,0:T(8,128)(2,1)}, bf16[4,256,512]{2,1,0:T(8,128)(2,1)S(1)}, u32[]{:S(2)}) copy-start(bf16[4,256,512]{2,1,0:T(8,128)(2,1)S(1)} %collective-permute-done.24.refs_5_) | copy-start | bytes 3145732
  109.9 27.1 %collective-permute-start.29 = (s16[608,128]{1,0:T(8,128)(2,1)}, s16[608,128]{1,0:T(8,128)(2,1)S(1)}, u32[]{:S(2)}, u32[]{:S(2)}) collective-permute-start(s16[608,128]{1,0:T(8,128)(2,1)} %get-tuple-element.20), channel_id=1, source_target_pairs={{128,0},{160,32},{192,64},{224,96},{0,128},{32,160},{64,192},{96,2... | collective-permute-start | bytes 466952 | tf_op jit(solution)/shard_map/ppermute | solution.py:37
  116.1 20.9 %collective-permute-start.30 = (s16[608,128]{1,0:T(8,128)(2,1)}, s16[608,128]{1,0:T(8,128)(2,1)S(1)}, u32[]{:S(2)}, u32[]{:S(2)}) collective-permute-start(s16[608,128]{1,0:T(8,128)(2,1)} %get-tuple-element.24), channel_id=1, source_target_pairs={{160,0},{192,32},{224,64},{0,96},{32,128},{64,160},{96,192},{128,2... | collective-permute-start | bytes 466952 | tf_op jit(solution)/shard_map/ppermute | solution.py:37
  116.1 23.7 %collective-permute-start.31 = (s16[608,128]{1,0:T(8,128)(2,1)}, s16[608,128]{1,0:T(8,128)(2,1)S(1)}, u32[]{:S(2)}, u32[]{:S(2)}) collective-permute-start(s16[608,128]{1,0:T(8,128)(2,1)} %get-tuple-element.25), channel_id=1, source_target_pairs={{96,0},{128,32},{160,64},{192,96},{224,128},{0,160},{32,192},{64,2... | collective-permute-start | bytes 466952 | tf_op jit(solution)/shard_map/ppermute | solution.py:37
  120.6 17.9 %copy-start.10 = (s32[4752]{0:T(1024)S(1)}, s32[4752]{0:T(1024)}, u32[]{:S(2)}) copy-start(s32[4752]{0:T(1024)} %param.10) | copy-start | bytes 57028
  120.6 18.0 %copy-start.6 = (s32[2048,8]{0,1:T(8,128)S(1)}, s32[2048,8]{0,1:T(8,128)}, u32[]{:S(2)}) copy-start(s32[2048,8]{0,1:T(8,128)} %param.11) | copy-start | bytes 196612
  120.6 19.3 %collective-permute-start.32 = (s16[608,128]{1,0:T(8,128)(2,1)}, s16[608,128]{1,0:T(8,128)(2,1)S(1)}, u32[]{:S(2)}, u32[]{:S(2)}) collective-permute-start(s16[608,128]{1,0:T(8,128)(2,1)} %get-tuple-element.26), channel_id=1, source_target_pairs={{192,0},{224,32},{0,64},{32,96},{64,128},{96,160},{128,192},{160,2... | collective-permute-start | bytes 466952 | tf_op jit(solution)/shard_map/ppermute | solution.py:37
  134.4 13.6 %copy-start.1 = (f32[608,128]{1,0:T(8,128)S(1)}, f32[608,128]{1,0:T(8,128)}, u32[]{:S(2)}) copy-start(f32[608,128]{1,0:T(8,128)} %get-tuple-element.23.own) | copy-start | bytes 933892
  134.4 9.2 %collective-permute-start.33 = (s16[608,128]{1,0:T(8,128)(2,1)}, s16[608,128]{1,0:T(8,128)(2,1)S(1)}, u32[]{:S(2)}, u32[]{:S(2)}) collective-permute-start(s16[608,128]{1,0:T(8,128)(2,1)} %get-tuple-element.27), channel_id=1, source_target_pairs={{64,0},{96,32},{128,64},{160,96},{192,128},{224,160},{0,192},{32,2... | collective-permute-start | bytes 466952 | tf_op jit(solution)/shard_map/ppermute | solution.py:37
  137.0 9.7 %collective-permute-start.34 = (s16[608,128]{1,0:T(8,128)(2,1)}, s16[608,128]{1,0:T(8,128)(2,1)S(1)}, u32[]{:S(2)}, u32[]{:S(2)}) collective-permute-start(s16[608,128]{1,0:T(8,128)(2,1)} %get-tuple-element.28), channel_id=1, source_target_pairs={{32,0},{64,32},{96,64},{128,96},{160,128},{192,160},{224,192},{0,2... | collective-permute-start | bytes 466952 | tf_op jit(solution)/shard_map/ppermute | solution.py:37
  137.0 10.3 %collective-permute-start.35 = (s16[608,128]{1,0:T(8,128)(2,1)}, s16[608,128]{1,0:T(8,128)(2,1)S(1)}, u32[]{:S(2)}, u32[]{:S(2)}) collective-permute-start(s16[608,128]{1,0:T(8,128)(2,1)} %get-tuple-element.29), channel_id=1, source_target_pairs={{224,0},{0,32},{32,64},{64,96},{96,128},{128,160},{160,192},{192,2... | collective-permute-start | bytes 466952 | tf_op jit(solution)/shard_map/ppermute | solution.py:37
  (11 other events, 29.8 us)
where the time goes:
time: 166 us
  starting transfers between devices  74.1 us (45%)
  waiting for transfers between devices  39.3 us (24%)
  Pallas kernels  25.7 us (15%)
  blocking collectives  12 us (7%)
  local copies, waits for them, and re-layouts  10.7 us (6%)
  other arithmetic  2.95 us (2%)
    ppermute x14, starting transfers between devices, from_row_group(): lax.ppermute(block, 'rows', [((k + offset) % count, k) for k in range(cou...  33.9 us
    ppermute x12, waiting for transfers between devices, sent(): return lax.ppermute(block, 'vocab', pairs)  28.4 us
    ppermute x10, starting transfers between devices, swapped(): return lax.ppermute(block, 'vocab', [(k, k ^ 1) for k in range(count)])  25.2 us
    pallas_call x2, Pallas kernels, group_logits(): pl.pallas_call(functools.partial(logits_body, keep=keep), out_shape=outs,...  22.7 us
    ppermute x12, starting transfers between devices, sent(): return lax.ppermute(block, 'vocab', pairs)  15 us
    all_to_all x1, blocking collectives, merged(): lax.all_to_all(copies, 'vocab', split_axis=0, concat_axis=0, tiled=True)  12 us
    ppermute x14, waiting for transfers between devices, from_row_group(): lax.ppermute(block, 'rows', [((k + offset) % count, k) for k in range(cou...  9.65 us
    unnamed x47, local copies, waits for them, and re-layouts  7.02 us
  transfers between devices with their start and end apart: 36, of which 12 were waited for; matrix products, arithmetic and copies ran while one was open for 3% of the time, Pallas kernels for 14%

commit v1 on v0

--- a/solution.py
+++ b/solution.py
@@ -165,21 +165,20 @@
     )(*blocks)
 
 
-def line_body(own, before, after, low, high, *outs):
-    for k, (out, last) in enumerate(zip(outs, (low, high))):
-        out[0] = own[k]
-        out[1] = before[k]
-        out[2] = after[k]
-        out[3] = last[0]
-
-
-def lines(own, *parts):
+def line_body(*refs):
+    parts, outs = refs[:4], refs[4:]
+    for k, out in enumerate(outs):
+        for at, part in enumerate(parts):
+            out[at] = part[k]
+
+
+def lines(*parts):
     return pl.pallas_call(
         line_body,
-        out_shape=[jax.ShapeDtypeStruct((4, *own.shape[1:]), own.dtype)] * 2,
+        out_shape=[jax.ShapeDtypeStruct((4, *parts[0].shape[1:]), parts[0].dtype)] * 2,
         compiler_params=pltpu.CompilerParams(vmem_limit_bytes=vmem_bytes),
         name="lines",
-    )(own, *parts)
+    )(*parts)
 
 
 def decode_body(place, mask, own, *refs, offsets):
@@ -278,8 +277,8 @@
     hidden_t = hidden.T
     found = [hidden_t if s == 0 else from_row_group(hidden_t, s) for s in (*far_offsets, *near_offsets)]
     block = ordered(found)
-    ends = ring_ends(block, True)
-    far_line, near_line = lines(block, *ends, *ring_far(*ends, True))
+    opposite = sent(block, plane_shift(True, 2))
+    far_line, near_line = lines(block, *ring_ends(block, True), opposite)
 
     head_t = head.T
     own_states = lax.dynamic_slice_in_dim(states, lax.axis_index("rows") * count, count, 0)

time: 166 us -> 160 us (0.964)
  starting transfers between devices: 74.1 us -> 62.2 us
  waiting for transfers between devices: 39.3 us -> 44.4 us
    ppermute x10, starting transfers between devices: 25.2 us -> 15.3 us  [swapped(): return lax.ppermute(block, 'vocab', [(k, k ^ 1) for k in range(count)])]
    ppermute x12 -> x11, waiting for transfers between devices: 28.4 us -> 33.5 us  [sent(): return lax.ppermute(block, 'vocab', pairs)]
    ppermute x12 -> x11, starting transfers between devices: 15 us -> 13.8 us  [sent(): return lax.ppermute(block, 'vocab', pairs)]
    slice x6 -> x4, local copies, waits for them, and re-layouts: 3.55 us -> 3.51 us  [ring_far(): low, high = (tied(before[:half], gate), tied(after[half:], gate))]
  transfers between devices with their start and end apart: 36 -> 35, of which waited for: 12 -> 12; matrix products, arithmetic and copies ran while one was open for 3% -> 3% of each run, Pallas kernels for 14% -> 15%
where the time goes in v1:
time: 160 us
  starting transfers between devices  62.2 us (39%)
  waiting for transfers between devices  44.4 us (28%)
  Pallas kernels  25.7 us (16%)
  blocking collectives  12.7 us (8%)
  local copies, waits for them, and re-layouts  10.7 us (7%)
  other arithmetic  2.93 us (2%)
    ppermute x11, waiting for transfers between devices, sent(): return lax.ppermute(block, 'vocab', pairs)  33.5 us
    ppermute x14, starting transfers between devices, from_row_group(): lax.ppermute(block, 'rows', [((k + offset) % count, k) for k in range(cou...  33.1 us
    pallas_call x2, Pallas kernels, group_logits(): pl.pallas_call(functools.partial(logits_body, keep=keep), out_shape=outs,...  22.6 us
    ppermute x10, starting transfers between devices, swapped(): return lax.ppermute(block, 'vocab', [(k, k ^ 1) for k in range(count)])  15.3 us
    ppermute x11, starting transfers between devices, sent(): return lax.ppermute(block, 'vocab', pairs)  13.8 us
    all_to_all x1, blocking collectives, merged(): lax.all_to_all(copies, 'vocab', split_axis=0, concat_axis=0, tiled=True)  12.7 us
    ppermute x14, waiting for transfers between devices, from_row_group(): lax.ppermute(block, 'rows', [((k + offset) % count, k) for k in range(cou...  9.64 us
    unnamed x47, local copies, waits for them, and re-layouts  7.03 us
  transfers between devices with their start and end apart: 35, of which 12 were waited for; matrix products, arithmetic and copies ran while one was open for 3% of the time, Pallas kernels for 15%

profile of v1, /device:TPU:1, one launch (start us, length us, event | category | flops | bytes accessed | tf_op | source)
XLA Modules:
  0.0 159.6 jit_solution(12569263796633495076)
XLA Ops:
  0.6 1.0 copy.13
  1.6 7.8 %collective-permute-start = (bf16[256,128]{1,0:T(8,128)(2,1)S(1)}, bf16[256,128]{1,0:T(8,128)(2,1)S(1)}, u32[]{:S(2)}, u32[]{:S(2)}) collective-permute-start(bf16[256,128]{1,0:T(8,128)(2,1)S(1)} %bitcast.16), channel_id=1, source_target_pairs={{128,0},{160,32},{192,64},{224,96},{0,128},{32,160},{64,192},{96,2... | collective-permute-start | bytes 196616 | tf_op jit(solution)/shard_map/ppermute | solution.py:37
  9.5 3.3 %collective-permute-start.2 = (bf16[256,128]{1,0:T(8,128)(2,1)S(1)}, bf16[256,128]{1,0:T(8,128)(2,1)S(1)}, u32[]{:S(2)}, u32[]{:S(2)}) collective-permute-start(bf16[256,128]{1,0:T(8,128)(2,1)S(1)} %bitcast.18), channel_id=1, source_target_pairs={{160,0},{192,32},{224,64},{0,96},{32,128},{64,160},{96,192},{128,2... | collective-permute-start | bytes 196616 | tf_op jit(solution)/shard_map/ppermute | solution.py:37
  13.5 1.6 %collective-permute-start.4 = (bf16[256,128]{1,0:T(8,128)(2,1)S(1)}, bf16[256,128]{1,0:T(8,128)(2,1)S(1)}, u32[]{:S(2)}, u32[]{:S(2)}) collective-permute-start(bf16[256,128]{1,0:T(8,128)(2,1)S(1)} %bitcast.20), channel_id=1, source_target_pairs={{192,0},{224,32},{0,64},{32,96},{64,128},{96,160},{128,192},{160,2... | collective-permute-start | bytes 196616 | tf_op jit(solution)/shard_map/ppermute | solution.py:37
  15.1 1.9 %collective-permute-start.5 = (bf16[256,128]{1,0:T(8,128)(2,1)S(1)}, bf16[256,128]{1,0:T(8,128)(2,1)S(1)}, u32[]{:S(2)}, u32[]{:S(2)}) collective-permute-start(bf16[256,128]{1,0:T(8,128)(2,1)S(1)} %bitcast.21), channel_id=1, source_target_pairs={{224,0},{0,32},{32,64},{64,96},{96,128},{128,160},{160,192},{192,2... | collective-permute-start | bytes 196616 | tf_op jit(solution)/shard_map/ppermute | solution.py:37
  17.0 2.4 %collective-permute-start.6 = (bf16[256,128]{1,0:T(8,128)(2,1)S(1)}, bf16[256,128]{1,0:T(8,128)(2,1)S(1)}, u32[]{:S(2)}, u32[]{:S(2)}) collective-permute-start(bf16[256,128]{1,0:T(8,128)(2,1)S(1)} %bitcast.22), channel_id=1, source_target_pairs={{32,0},{64,32},{96,64},{128,96},{160,128},{192,160},{224,192},{0,2... | collective-permute-start | bytes 196616 | tf_op jit(solution)/shard_map/ppermute | solution.py:37
  19.4 1.0 collective-permute-done.3.refs_3_
  20.5 1.8 %collective-permute-done.5.refs_5_ = bf16[256,128]{1,0:T(8,128)(2,1)S(1)} collective-permute-done((bf16[256,128]{1,0:T(8,128)(2,1)S(1)}, bf16[256,128]{1,0:T(8,128)(2,1)S(1)}, u32[]{:S(2)}, u32[]{:S(2)}) %collective-permute-start.5) | collective-permute-done | bytes 65568 | tf_op jit(solution)/shard_map/ppermute | solution.py:37
  22.4 1.2 collective-permute-start.7
  23.6 1.5 collective-permute-start.8
  25.2 1.6 collective-permute-start.9
  26.7 5.3 %collective-permute-done.7.refs_1_ = bf16[2,256,512]{2,1,0:T(8,128)(2,1)S(1)} collective-permute-done((bf16[2,256,512]{2,1,0:T(8,128)(2,1)S(1)}, bf16[2,256,512]{2,1,0:T(8,128)(2,1)S(1)}, u32[]{:S(2)}, u32[]{:S(2)}) %collective-permute-start.7) | collective-permute-done | bytes 524320 | tf_op jit(solution)/shard_map/ppermute | solution.py:32
  32.0 4.9 %collective-permute-done.8.refs_2_ = bf16[2,256,512]{2,1,0:T(8,128)(2,1)S(1)} collective-permute-done((bf16[2,256,512]{2,1,0:T(8,128)(2,1)S(1)}, bf16[2,256,512]{2,1,0:T(8,128)(2,1)S(1)}, u32[]{:S(2)}, u32[]{:S(2)}) %collective-permute-start.8) | collective-permute-done | bytes 524320 | tf_op jit(solution)/shard_map/ppermute | solution.py:32
  36.9 1.8 %collective-permute-done.9.refs_3_ = bf16[2,256,512]{2,1,0:T(8,128)(2,1)S(1)} collective-permute-done((bf16[2,256,512]{2,1,0:T(8,128)(2,1)S(1)}, bf16[2,256,512]{2,1,0:T(8,128)(2,1)S(1)}, u32[]{:S(2)}, u32[]{:S(2)}) %collective-permute-start.9) | collective-permute-done | bytes 524320 | tf_op jit(solution)/shard_map/ppermute | solution.py:32
  38.9 1.0 collective-permute-start.10
  39.9 1.8 %collective-permute-start.12 = (bf16[4,256,512]{2,1,0:T(8,128)(2,1)S(1)}, bf16[4,256,512]{2,1,0:T(8,128)(2,1)}, u32[]{:S(2)}, u32[]{:S(2)}) collective-permute-start(bf16[4,256,512]{2,1,0:T(8,128)(2,1)S(1)} %get-tuple-element.18.refs_0_), channel_id=1, source_target_pairs={{0,24},{1,7},{2,26},{3,1},{4,28},{5,3},{6,30},{7,5},{8,0},{9,15},{... | collective-permute-start | bytes 3145736 | tf_op jit(solution)/shard_map/ppermute | solution.py:32
  41.7 2.9 %collective-permute-start.16 = (bf16[4,256,512]{2,1,0:T(8,128)(2,1)S(1)}, bf16[4,256,512]{2,1,0:T(8,128)(2,1)S(1)}, u32[]{:S(2)}, u32[]{:S(2)}) collective-permute-start(bf16[4,256,512]{2,1,0:T(8,128)(2,1)S(1)} %get-tuple-element.18.refs_0_), channel_id=1, source_target_pairs={{0,1},{1,0},{2,3},{3,2},{4,5},{5,4},{6,7},{7,6},{8,9},{9,8},{10,11... | collective-permute-start | bytes 3145736 | tf_op jit(solution)/shard_map/ppermute | solution.py:42
  44.5 9.6 %collective-permute-done.10.refs_1_ = bf16[4,256,512]{2,1,0:T(8,128)(2,1)S(1)} collective-permute-done((bf16[4,256,512]{2,1,0:T(8,128)(2,1)S(1)}, bf16[4,256,512]{2,1,0:T(8,128)(2,1)S(1)}, u32[]{:S(2)}, u32[]{:S(2)}) %collective-permute-start.10) | collective-permute-done | bytes 1048608 | tf_op jit(solution)/shard_map/ppermute | solution.py:32
  54.3 1.3 slice.30
  55.6 2.5 %collective-permute-start.13 = (bf16[2,256,512]{2,1,0:T(8,128)(2,1)S(1)}, bf16[2,256,512]{2,1,0:T(8,128)(2,1)}, u32[]{:S(2)}, u32[]{:S(2)}) collective-permute-start(bf16[2,256,512]{2,1,0:T(8,128)(2,1)S(1)} %slice.30), channel_id=1, source_target_pairs={{0,24},{1,7},{2,26},{3,1},{4,28},{5,3},{6,30},{7,5},{8,0},{9,15},{... | collective-permute-start | bytes 1572872 | tf_op jit(solution)/shard_map/ppermute | solution.py:32
  58.1 5.7 %collective-permute-done.11.refs_3_ = bf16[2,256,512]{2,1,0:T(8,128)(2,1)S(1)} collective-permute-done((bf16[2,256,512]{2,1,0:T(8,128)(2,1)S(1)}, bf16[2,256,512]{2,1,0:T(8,128)(2,1)S(1)}, u32[]{:S(2)}, u32[]{:S(2)}) %collective-permute-start.11) | collective-permute-done | bytes 524320 | tf_op jit(solution)/shard_map/ppermute | solution.py:32
  63.8 4.0 %collective-permute-start.19 = (bf16[2,256,512]{2,1,0:T(8,128)(2,1)S(1)}, bf16[2,256,512]{2,1,0:T(8,128)(2,1)S(1)}, u32[]{:S(2)}, u32[]{:S(2)}) collective-permute-start(bf16[2,256,512]{2,1,0:T(8,128)(2,1)S(1)} %collective-permute-done.11.refs_3_), channel_id=1, source_target_pairs={{0,1},{1,0},{2,3},{3,2},{4,5},{5,4},{6,7},{7,6},{8,9},{9,8},{10,11... | collective-permute-start | bytes 1572872 | tf_op jit(solution)/shard_map/ppermute | solution.py:42
  68.3 2.0 %collective-permute-start.15 = (bf16[4,256,512]{2,1,0:T(8,128)(2,1)S(1)}, bf16[4,256,512]{2,1,0:T(8,128)(2,1)}, u32[]{:S(2)}, u32[]{:S(2)}) collective-permute-start(bf16[4,256,512]{2,1,0:T(8,128)(2,1)S(1)} %get-tuple-element.19.refs_0_), channel_id=1, source_target_pairs={{0,24},{1,7},{2,26},{3,1},{4,28},{5,3},{6,30},{7,5},{8,0},{9,15},{... | collective-permute-start | bytes 3145736 | tf_op jit(solution)/shard_map/ppermute | solution.py:32
  70.3 1.1 copy-done.13
  72.2 2.0 %collective-permute-start.20 = (bf16[2,256,512]{2,1,0:T(8,128)(2,1)}, bf16[2,256,512]{2,1,0:T(8,128)(2,1)}, u32[]{:S(2)}, u32[]{:S(2)}) collective-permute-start(bf16[2,256,512]{2,1,0:T(8,128)(2,1)} %collective-permute-done.13.refs_4_), channel_id=1, source_target_pairs={{0,1},{1,0},{2,3},{3,2},{4,5},{5,4},{6,7},{7,6},{8,9},{9,8},{10,11... | collective-permute-start | bytes 1572872 | tf_op jit(solution)/shard_map/ppermute | solution.py:42
  74.9 1.2 collective-permute-done.20.refs_9_
  76.5 11.3 %group_logits.2 = (s16[608,128]{1,0:T(8,128)(2,1)}, s16[608,128]{1,0:T(8,128)(2,1)}, s16[608,128]{1,0:T(8,128)(2,1)}, s16[608,128]{1,0:T(8,128)(2,1)}) custom-call(s32[17]{0:T(128)} %pad_add_fusion.numbers, bf16[4,256,512]{2,1,0:T(8,128)(2,1)} %copy-done.8, bf16[4,256,512]{2,1,0:T(8,128)(2,1)} %copy-done.9, ...), custom_call_target="tpu_custom_call" | custom-call | flops 4982833152 | bytes 9732096 | tf_op jit(solution)/shard_map/group_logits/pallas_call | solution.py:133
  87.8 1.1 slice.32
  88.9 2.1 %collective-permute-start.22 = (bf16[2,256,512]{2,1,0:T(8,128)(2,1)S(1)}, bf16[2,256,512]{2,1,0:T(8,128)(2,1)S(1)}, u32[]{:S(2)}, u32[]{:S(2)}) collective-permute-start(bf16[2,256,512]{2,1,0:T(8,128)(2,1)S(1)} %slice.32), channel_id=1, source_target_pairs={{0,24},{1,7},{2,26},{3,1},{4,28},{5,3},{6,30},{7,5},{8,0},{9,15},{... | collective-permute-start | bytes 1572872 | tf_op jit(solution)/shard_map/ppermute | solution.py:32
  90.9 1.1 slice.31
  92.1 1.5 collective-permute-start.24
  93.7 3.6 %collective-permute-done.22.refs_4_ = bf16[2,256,512]{2,1,0:T(8,128)(2,1)S(1)} collective-permute-done((bf16[2,256,512]{2,1,0:T(8,128)(2,1)S(1)}, bf16[2,256,512]{2,1,0:T(8,128)(2,1)S(1)}, u32[]{:S(2)}, u32[]{:S(2)}) %collective-permute-start.22) | collective-permute-done | bytes 524320 | tf_op jit(solution)/shard_map/ppermute | solution.py:32
  97.3 1.7 %collective-permute-start.27 = (bf16[2,256,512]{2,1,0:T(8,128)(2,1)S(1)}, bf16[2,256,512]{2,1,0:T(8,128)(2,1)S(1)}, u32[]{:S(2)}, u32[]{:S(2)}) collective-permute-start(bf16[2,256,512]{2,1,0:T(8,128)(2,1)S(1)} %collective-permute-done.22.refs_4_), channel_id=1, source_target_pairs={{0,1},{1,0},{2,3},{3,2},{4,5},{5,4},{6,7},{7,6},{8,9},{9,8},{10,11... | collective-permute-start | bytes 1572872 | tf_op jit(solution)/shard_map/ppermute | solution.py:42
  99.0 2.6 %collective-permute-done.21.refs_3_ = bf16[2,256,512]{2,1,0:T(8,128)(2,1)S(1)} collective-permute-done((bf16[2,256,512]{2,1,0:T(8,128)(2,1)S(1)}, bf16[2,256,512]{2,1,0:T(8,128)(2,1)S(1)}, u32[]{:S(2)}, u32[]{:S(2)}) %collective-permute-start.21) | collective-permute-done | bytes 524320 | tf_op jit(solution)/shard_map/ppermute | solution.py:32
  101.6 2.2 %collective-permute-start.26 = (bf16[2,256,512]{2,1,0:T(8,128)(2,1)S(1)}, bf16[2,256,512]{2,1,0:T(8,128)(2,1)S(1)}, u32[]{:S(2)}, u32[]{:S(2)}) collective-permute-start(bf16[2,256,512]{2,1,0:T(8,128)(2,1)S(1)} %collective-permute-done.21.refs_3_), channel_id=1, source_target_pairs={{0,1},{1,0},{2,3},{3,2},{4,5},{5,4},{6,7},{7,6},{8,9},{9,8},{10,11... | collective-permute-start | bytes 1572872 | tf_op jit(solution)/shard_map/ppermute | solution.py:42
  103.9 5.5 %collective-permute-start.28 = (s16[608,128]{1,0:T(8,128)(2,1)}, s16[608,128]{1,0:T(8,128)(2,1)S(1)}, u32[]{:S(2)}, u32[]{:S(2)}) collective-permute-start(s16[608,128]{1,0:T(8,128)(2,1)} %get-tuple-element.20), channel_id=1, source_target_pairs={{128,0},{160,32},{192,64},{224,96},{0,128},{32,160},{64,192},{96,2... | collective-permute-start | bytes 466952 | tf_op jit(solution)/shard_map/ppermute | solution.py:37
  109.5 4.3 %collective-permute-start.30 = (s16[608,128]{1,0:T(8,128)(2,1)}, s16[608,128]{1,0:T(8,128)(2,1)S(1)}, u32[]{:S(2)}, u32[]{:S(2)}) collective-permute-start(s16[608,128]{1,0:T(8,128)(2,1)} %get-tuple-element.25), channel_id=1, source_target_pairs={{96,0},{128,32},{160,64},{192,96},{224,128},{0,160},{32,192},{64,2... | collective-permute-start | bytes 466952 | tf_op jit(solution)/shard_map/ppermute | solution.py:37
  113.8 1.4 collective-permute-start.31
  115.3 1.0 copy-done.16
  116.3 11.3 %group_logits.3 = (s16[608,128]{1,0:T(8,128)(2,1)}, s16[608,128]{1,0:T(8,128)(2,1)}, s16[608,128]{1,0:T(8,128)(2,1)}, f32[608,128]{1,0:T(8,128)}) custom-call(s32[17]{0:T(128)} %pad_add_fusion.numbers, bf16[4,256,512]{2,1,0:T(8,128)(2,1)} %copy-done.7, bf16[4,256,512]{2,1,0:T(8,128)(2,1)} %collective-permute-done.14.refs_1_, ...), custom_call_target="tpu_custom_call" | custom-call | flops 4982833152 | bytes 9732096 | tf_op jit(solution)/shard_map/group_logits/pallas_call | solution.py:133
  127.7 2.5 %collective-permute-start.32 = (s16[608,128]{1,0:T(8,128)(2,1)}, s16[608,128]{1,0:T(8,128)(2,1)S(1)}, u32[]{:S(2)}, u32[]{:S(2)}) collective-permute-start(s16[608,128]{1,0:T(8,128)(2,1)} %get-tuple-element.27), channel_id=1, source_target_pairs={{64,0},{96,32},{128,64},{160,96},{192,128},{224,160},{0,192},{32,2... | collective-permute-start | bytes 466952 | tf_op jit(solution)/shard_map/ppermute | solution.py:37
  130.2 1.5 collective-permute-start.34
  131.8 1.3 mask.1
  133.1 4.0 %collective-permute-done.32.refs_4_ = s16[608,128]{1,0:T(8,128)(2,1)S(1)} collective-permute-done((s16[608,128]{1,0:T(8,128)(2,1)}, s16[608,128]{1,0:T(8,128)(2,1)S(1)}, u32[]{:S(2)}, u32[]{:S(2)}) %collective-permute-start.32) | collective-permute-done | bytes 155680 | tf_op jit(solution)/shard_map/ppermute | solution.py:37
  137.1 2.7 %collective-permute-done.33.refs_5_ = s16[608,128]{1,0:T(8,128)(2,1)S(1)} collective-permute-done((s16[608,128]{1,0:T(8,128)(2,1)}, s16[608,128]{1,0:T(8,128)(2,1)S(1)}, u32[]{:S(2)}, u32[]{:S(2)}) %collective-permute-start.33) | collective-permute-done | bytes 155680 | tf_op jit(solution)/shard_map/ppermute | solution.py:37
  143.0 1.6 decode.1
  144.6 12.7 %all_to_all.5 = f32[32,3,128]{2,1,0:T(4,128)S(1)} all-to-all(f32[32,3,128]{2,1,0:T(4,128)S(1)} %broadcast_in_dim.9), channel_id=1, replica_groups=mesh['rows'=8,'vocab'=32] {'vocab'}, dimensions={0} | all-to-all | bytes 98304 | tf_op jit(solution)/shard_map/all_to_all | solution.py:266
  157.9 1.7 %select_bitcast_fusion = f32[128,4752]{0,1:T(8,128)} fusion(f32[4752,128]{1,0:T(8,128)S(1)} %get-tuple-element.30, f32[128]{0:T(128)S(1)} %get-tuple-element.38), kind=kLoop, calls=%fused_computation | loop fusion | flops 1824768 | bytes 4866560 | tf_op jit(solution)/shard_map/transpose | solution.py:309
  (91 shorter events, 7.8 us)
Async XLA Ops:
  0.6 131.1 %copy-start = (s32[1024]{0:T(1024)S(1)}, s32[1024]{0:T(1024)}, u32[]{:S(2)}) copy-start(s32[1024]{0:T(1024)} %param.9) | copy-start | bytes 12292
  1.6 72.6 %copy-start.11 = (s32[16]{0:T(128)S(1)}, s32[16]{0:T(128)}, u32[]{:S(2)}) copy-start(s32[16]{0:T(128)} %constant.82.clone) | copy-start | bytes 196
  1.6 72.6 %copy-start.12 = (s32[16]{0:T(128)S(1)}, s32[16]{0:T(128)}, u32[]{:S(2)}) copy-start(s32[16]{0:T(128)} %constant.83.clone) | copy-start | bytes 196
  1.6 13.5 %collective-permute-start = (bf16[256,128]{1,0:T(8,128)(2,1)S(1)}, bf16[256,128]{1,0:T(8,128)(2,1)S(1)}, u32[]{:S(2)}, u32[]{:S(2)}) collective-permute-start(bf16[256,128]{1,0:T(8,128)(2,1)S(1)} %bitcast.16), channel_id=1, source_target_pairs={{128,0},{160,32},{192,64},{224,96},{0,128},{32,160},{64,192},{96,2... | collective-permute-start | bytes 196616 | tf_op jit(solution)/shard_map/ppermute | solution.py:37
  9.5 7.6 %collective-permute-start.1 = (bf16[256,128]{1,0:T(8,128)(2,1)S(1)}, bf16[256,128]{1,0:T(8,128)(2,1)S(1)}, u32[]{:S(2)}, u32[]{:S(2)}) collective-permute-start(bf16[256,128]{1,0:T(8,128)(2,1)S(1)} %bitcast.17), channel_id=1, source_target_pairs={{96,0},{128,32},{160,64},{192,96},{224,128},{0,160},{32,192},{64,2... | collective-permute-start | bytes 196616 | tf_op jit(solution)/shard_map/ppermute | solution.py:37
  9.5 10.0 %collective-permute-start.2 = (bf16[256,128]{1,0:T(8,128)(2,1)S(1)}, bf16[256,128]{1,0:T(8,128)(2,1)S(1)}, u32[]{:S(2)}, u32[]{:S(2)}) collective-permute-start(bf16[256,128]{1,0:T(8,128)(2,1)S(1)} %bitcast.18), channel_id=1, source_target_pairs={{160,0},{192,32},{224,64},{0,96},{32,128},{64,160},{96,192},{128,2... | collective-permute-start | bytes 196616 | tf_op jit(solution)/shard_map/ppermute | solution.py:37
  12.7 7.7 %collective-permute-start.3 = (bf16[256,128]{1,0:T(8,128)(2,1)S(1)}, bf16[256,128]{1,0:T(8,128)(2,1)S(1)}, u32[]{:S(2)}, u32[]{:S(2)}) collective-permute-start(bf16[256,128]{1,0:T(8,128)(2,1)S(1)} %bitcast.19), channel_id=1, source_target_pairs={{64,0},{96,32},{128,64},{160,96},{192,128},{224,160},{0,192},{32,2... | collective-permute-start | bytes 196616 | tf_op jit(solution)/shard_map/ppermute | solution.py:37
  13.5 7.0 %collective-permute-start.4 = (bf16[256,128]{1,0:T(8,128)(2,1)S(1)}, bf16[256,128]{1,0:T(8,128)(2,1)S(1)}, u32[]{:S(2)}, u32[]{:S(2)}) collective-permute-start(bf16[256,128]{1,0:T(8,128)(2,1)S(1)} %bitcast.20), channel_id=1, source_target_pairs={{192,0},{224,32},{0,64},{32,96},{64,128},{96,160},{128,192},{160,2... | collective-permute-start | bytes 196616 | tf_op jit(solution)/shard_map/ppermute | solution.py:37
  15.1 7.2 %collective-permute-start.5 = (bf16[256,128]{1,0:T(8,128)(2,1)S(1)}, bf16[256,128]{1,0:T(8,128)(2,1)S(1)}, u32[]{:S(2)}, u32[]{:S(2)}) collective-permute-start(bf16[256,128]{1,0:T(8,128)(2,1)S(1)} %bitcast.21), channel_id=1, source_target_pairs={{224,0},{0,32},{32,64},{64,96},{96,128},{128,160},{160,192},{192,2... | collective-permute-start | bytes 196616 | tf_op jit(solution)/shard_map/ppermute | solution.py:37
  17.0 5.3 %collective-permute-start.6 = (bf16[256,128]{1,0:T(8,128)(2,1)S(1)}, bf16[256,128]{1,0:T(8,128)(2,1)S(1)}, u32[]{:S(2)}, u32[]{:S(2)}) collective-permute-start(bf16[256,128]{1,0:T(8,128)(2,1)S(1)} %bitcast.22), channel_id=1, source_target_pairs={{32,0},{64,32},{96,64},{128,96},{160,128},{192,160},{224,192},{0,2... | collective-permute-start | bytes 196616 | tf_op jit(solution)/shard_map/ppermute | solution.py:37
  22.4 9.6 %collective-permute-start.7 = (bf16[2,256,512]{2,1,0:T(8,128)(2,1)S(1)}, bf16[2,256,512]{2,1,0:T(8,128)(2,1)S(1)}, u32[]{:S(2)}, u32[]{:S(2)}) collective-permute-start(bf16[2,256,512]{2,1,0:T(8,128)(2,1)S(1)} %ordered.1.refs_0_), channel_id=1, source_target_pairs={{0,2},{1,9},{2,4},{3,11},{4,6},{5,13},{6,0},{7,15},{8,10},{9,17},{... | collective-permute-start | bytes 1572872 | tf_op jit(solution)/shard_map/ppermute | solution.py:32
  23.6 13.3 %collective-permute-start.8 = (bf16[2,256,512]{2,1,0:T(8,128)(2,1)S(1)}, bf16[2,256,512]{2,1,0:T(8,128)(2,1)S(1)}, u32[]{:S(2)}, u32[]{:S(2)}) collective-permute-start(bf16[2,256,512]{2,1,0:T(8,128)(2,1)S(1)} %ordered.1.refs_0_), channel_id=1, source_target_pairs={{0,6},{1,25},{2,0},{3,27},{4,2},{5,29},{6,4},{7,31},{8,14},{9,1},{... | collective-permute-start | bytes 1572872 | tf_op jit(solution)/shard_map/ppermute | solution.py:32
  25.2 13.6 %collective-permute-start.9 = (bf16[2,256,512]{2,1,0:T(8,128)(2,1)S(1)}, bf16[2,256,512]{2,1,0:T(8,128)(2,1)S(1)}, u32[]{:S(2)}, u32[]{:S(2)}) collective-permute-start(bf16[2,256,512]{2,1,0:T(8,128)(2,1)S(1)} %ordered.1.refs_0_), channel_id=1, source_target_pairs={{0,4},{1,17},{2,6},{3,19},{4,0},{5,21},{6,2},{7,23},{8,12},{9,25},... | collective-permute-start | bytes 1572872 | tf_op jit(solution)/shard_map/ppermute | solution.py:32
  38.9 37.6 %copy-start.8 = (bf16[4,256,512]{2,1,0:T(8,128)(2,1)}, bf16[4,256,512]{2,1,0:T(8,128)(2,1)S(1)}, u32[]{:S(2)}) copy-start(bf16[4,256,512]{2,1,0:T(8,128)(2,1)S(1)} %get-tuple-element.18.refs_0_) | copy-start | bytes 3145732
  38.9 48.9 %copy-start.7 = (bf16[4,256,512]{2,1,0:T(8,128)(2,1)}, bf16[4,256,512]{2,1,0:T(8,128)(2,1)S(1)}, u32[]{:S(2)}) copy-start(bf16[4,256,512]{2,1,0:T(8,128)(2,1)S(1)} %get-tuple-element.19.refs_0_) | copy-start | bytes 3145732
  38.9 15.2 %collective-permute-start.10 = (bf16[4,256,512]{2,1,0:T(8,128)(2,1)S(1)}, bf16[4,256,512]{2,1,0:T(8,128)(2,1)S(1)}, u32[]{:S(2)}, u32[]{:S(2)}) collective-permute-start(bf16[4,256,512]{2,1,0:T(8,128)(2,1)S(1)} %get-tuple-element.18.refs_0_), channel_id=1, source_target_pairs={{0,8},{1,3},{2,10},{3,5},{4,12},{5,7},{6,14},{7,1},{8,16},{9,11},{... | collective-permute-start | bytes 3145736 | tf_op jit(solution)/shard_map/ppermute | solution.py:32
  39.9 14.4 %collective-permute-start.12 = (bf16[4,256,512]{2,1,0:T(8,128)(2,1)S(1)}, bf16[4,256,512]{2,1,0:T(8,128)(2,1)}, u32[]{:S(2)}, u32[]{:S(2)}) collective-permute-start(bf16[4,256,512]{2,1,0:T(8,128)(2,1)S(1)} %get-tuple-element.18.refs_0_), channel_id=1, source_target_pairs={{0,24},{1,7},{2,26},{3,1},{4,28},{5,3},{6,30},{7,5},{8,0},{9,15},{... | collective-permute-start | bytes 3145736 | tf_op jit(solution)/shard_map/ppermute | solution.py:32
  41.7 28.6 %collective-permute-start.16 = (bf16[4,256,512]{2,1,0:T(8,128)(2,1)S(1)}, bf16[4,256,512]{2,1,0:T(8,128)(2,1)S(1)}, u32[]{:S(2)}, u32[]{:S(2)}) collective-permute-start(bf16[4,256,512]{2,1,0:T(8,128)(2,1)S(1)} %get-tuple-element.18.refs_0_), channel_id=1, source_target_pairs={{0,1},{1,0},{2,3},{3,2},{4,5},{5,4},{6,7},{7,6},{8,9},{9,8},{10,11... | collective-permute-start | bytes 3145736 | tf_op jit(solution)/shard_map/ppermute | solution.py:42
  54.1 22.3 %copy-start.9 = (bf16[4,256,512]{2,1,0:T(8,128)(2,1)}, bf16[4,256,512]{2,1,0:T(8,128)(2,1)S(1)}, u32[]{:S(2)}) copy-start(bf16[4,256,512]{2,1,0:T(8,128)(2,1)S(1)} %collective-permute-done.10.refs_1_) | copy-start | bytes 3145732
  54.2 9.6 %collective-permute-start.11 = (bf16[2,256,512]{2,1,0:T(8,128)(2,1)S(1)}, bf16[2,256,512]{2,1,0:T(8,128)(2,1)S(1)}, u32[]{:S(2)}, u32[]{:S(2)}) collective-permute-start(bf16[2,256,512]{2,1,0:T(8,128)(2,1)S(1)} %slice.29), channel_id=1, source_target_pairs={{0,8},{1,3},{2,10},{3,5},{4,12},{5,7},{6,14},{7,1},{8,16},{9,11},{... | collective-permute-start | bytes 1572872 | tf_op jit(solution)/shard_map/ppermute | solution.py:32
  55.6 12.7 %collective-permute-start.13 = (bf16[2,256,512]{2,1,0:T(8,128)(2,1)S(1)}, bf16[2,256,512]{2,1,0:T(8,128)(2,1)}, u32[]{:S(2)}, u32[]{:S(2)}) collective-permute-start(bf16[2,256,512]{2,1,0:T(8,128)(2,1)S(1)} %slice.30), channel_id=1, source_target_pairs={{0,24},{1,7},{2,26},{3,1},{4,28},{5,3},{6,30},{7,5},{8,0},{9,15},{... | collective-permute-start | bytes 1572872 | tf_op jit(solution)/shard_map/ppermute | solution.py:32
  63.8 7.6 %copy-start.17 = (bf16[2,256,512]{2,1,0:T(8,128)(2,1)}, bf16[2,256,512]{2,1,0:T(8,128)(2,1)S(1)}, u32[]{:S(2)}) copy-start(bf16[2,256,512]{2,1,0:T(8,128)(2,1)S(1)} %collective-permute-done.11.refs_3_) | copy-start | bytes 1572868
  63.8 7.6 %collective-permute-start.19 = (bf16[2,256,512]{2,1,0:T(8,128)(2,1)S(1)}, bf16[2,256,512]{2,1,0:T(8,128)(2,1)S(1)}, u32[]{:S(2)}, u32[]{:S(2)}) collective-permute-start(bf16[2,256,512]{2,1,0:T(8,128)(2,1)S(1)} %collective-permute-done.11.refs_3_), channel_id=1, source_target_pairs={{0,1},{1,0},{2,3},{3,2},{4,5},{5,4},{6,7},{7,6},{8,9},{9,8},{10,11... | collective-permute-start | bytes 1572872 | tf_op jit(solution)/shard_map/ppermute | solution.py:42
  67.8 8.6 %collective-permute-start.17 = (bf16[4,256,512]{2,1,0:T(8,128)(2,1)S(1)}, bf16[4,256,512]{2,1,0:T(8,128)(2,1)}, u32[]{:S(2)}, u32[]{:S(2)}) collective-permute-start(bf16[4,256,512]{2,1,0:T(8,128)(2,1)S(1)} %collective-permute-done.10.refs_1_), channel_id=1, source_target_pairs={{0,1},{1,0},{2,3},{3,2},{4,5},{5,4},{6,7},{7,6},{8,9},{9,8},{10,11... | collective-permute-start | bytes 3145736 | tf_op jit(solution)/shard_map/ppermute | solution.py:42
  67.8 8.6 %collective-permute-start.18 = (bf16[4,256,512]{2,1,0:T(8,128)(2,1)}, bf16[4,256,512]{2,1,0:T(8,128)(2,1)}, u32[]{:S(2)}, u32[]{:S(2)}) collective-permute-start(bf16[4,256,512]{2,1,0:T(8,128)(2,1)} %collective-permute-done.12.refs_2_), channel_id=1, source_target_pairs={{0,1},{1,0},{2,3},{3,2},{4,5},{5,4},{6,7},{7,6},{8,9},{9,8},{10,11... | collective-permute-start | bytes 3145736 | tf_op jit(solution)/shard_map/ppermute | solution.py:42
  68.3 19.5 %collective-permute-start.15 = (bf16[4,256,512]{2,1,0:T(8,128)(2,1)S(1)}, bf16[4,256,512]{2,1,0:T(8,128)(2,1)}, u32[]{:S(2)}, u32[]{:S(2)}) collective-permute-start(bf16[4,256,512]{2,1,0:T(8,128)(2,1)S(1)} %get-tuple-element.19.refs_0_), channel_id=1, source_target_pairs={{0,24},{1,7},{2,26},{3,1},{4,28},{5,3},{6,30},{7,5},{8,0},{9,15},{... | collective-permute-start | bytes 3145736 | tf_op jit(solution)/shard_map/ppermute | solution.py:32
  71.3 19.6 %collective-permute-start.14 = (bf16[4,256,512]{2,1,0:T(8,128)(2,1)S(1)}, bf16[4,256,512]{2,1,0:T(8,128)(2,1)}, u32[]{:S(2)}, u32[]{:S(2)}) collective-permute-start(bf16[4,256,512]{2,1,0:T(8,128)(2,1)S(1)} %get-tuple-element.19.refs_0_), channel_id=1, source_target_pairs={{0,8},{1,3},{2,10},{3,5},{4,12},{5,7},{6,14},{7,1},{8,16},{9,11},{... | collective-permute-start | bytes 3145736 | tf_op jit(solution)/shard_map/ppermute | solution.py:32
  72.2 3.9 %collective-permute-start.20 = (bf16[2,256,512]{2,1,0:T(8,128)(2,1)}, bf16[2,256,512]{2,1,0:T(8,128)(2,1)}, u32[]{:S(2)}, u32[]{:S(2)}) collective-permute-start(bf16[2,256,512]{2,1,0:T(8,128)(2,1)} %collective-permute-done.13.refs_4_), channel_id=1, source_target_pairs={{0,1},{1,0},{2,3},{3,2},{4,5},{5,4},{6,7},{7,6},{8,9},{9,8},{10,11... | collective-permute-start | bytes 1572872 | tf_op jit(solution)/shard_map/ppermute | solution.py:42
  76.1 27.8 %collective-permute-start.23 = (bf16[4,256,512]{2,1,0:T(8,128)(2,1)S(1)}, bf16[4,256,512]{2,1,0:T(8,128)(2,1)S(1)}, u32[]{:S(2)}, u32[]{:S(2)}) collective-permute-start(bf16[4,256,512]{2,1,0:T(8,128)(2,1)S(1)} %get-tuple-element.19.refs_0_), channel_id=1, source_target_pairs={{0,1},{1,0},{2,3},{3,2},{4,5},{5,4},{6,7},{7,6},{8,9},{9,8},{10,11... | collective-permute-start | bytes 3145736 | tf_op jit(solution)/shard_map/ppermute | solution.py:42
  88.9 8.4 %collective-permute-start.22 = (bf16[2,256,512]{2,1,0:T(8,128)(2,1)S(1)}, bf16[2,256,512]{2,1,0:T(8,128)(2,1)S(1)}, u32[]{:S(2)}, u32[]{:S(2)}) collective-permute-start(bf16[2,256,512]{2,1,0:T(8,128)(2,1)S(1)} %slice.32), channel_id=1, source_target_pairs={{0,24},{1,7},{2,26},{3,1},{4,28},{5,3},{6,30},{7,5},{8,0},{9,15},{... | collective-permute-start | bytes 1572872 | tf_op jit(solution)/shard_map/ppermute | solution.py:32
  92.0 9.6 %collective-permute-start.21 = (bf16[2,256,512]{2,1,0:T(8,128)(2,1)S(1)}, bf16[2,256,512]{2,1,0:T(8,128)(2,1)S(1)}, u32[]{:S(2)}, u32[]{:S(2)}) collective-permute-start(bf16[2,256,512]{2,1,0:T(8,128)(2,1)S(1)} %slice.31), channel_id=1, source_target_pairs={{0,8},{1,3},{2,10},{3,5},{4,12},{5,7},{6,14},{7,1},{8,16},{9,11},{... | collective-permute-start | bytes 1572872 | tf_op jit(solution)/shard_map/ppermute | solution.py:32
  92.1 21.7 %collective-permute-start.24 = (bf16[4,256,512]{2,1,0:T(8,128)(2,1)}, bf16[4,256,512]{2,1,0:T(8,128)(2,1)S(1)}, u32[]{:S(2)}, u32[]{:S(2)}) collective-permute-start(bf16[4,256,512]{2,1,0:T(8,128)(2,1)} %collective-permute-done.14.refs_1_), channel_id=1, source_target_pairs={{0,1},{1,0},{2,3},{3,2},{4,5},{5,4},{6,7},{7,6},{8,9},{9,8},{10,11... | collective-permute-start | bytes 3145736 | tf_op jit(solution)/shard_map/ppermute | solution.py:42
  93.6 21.7 %collective-permute-start.25 = (bf16[4,256,512]{2,1,0:T(8,128)(2,1)}, bf16[4,256,512]{2,1,0:T(8,128)(2,1)S(1)}, u32[]{:S(2)}, u32[]{:S(2)}) collective-permute-start(bf16[4,256,512]{2,1,0:T(8,128)(2,1)} %collective-permute-done.15.refs_2_), channel_id=1, source_target_pairs={{0,1},{1,0},{2,3},{3,2},{4,5},{5,4},{6,7},{7,6},{8,9},{9,8},{10,11... | collective-permute-start | bytes 3145736 | tf_op jit(solution)/shard_map/ppermute | solution.py:42
  97.3 18.0 %copy-start.19 = (bf16[2,256,512]{2,1,0:T(8,128)(2,1)}, bf16[2,256,512]{2,1,0:T(8,128)(2,1)S(1)}, u32[]{:S(2)}) copy-start(bf16[2,256,512]{2,1,0:T(8,128)(2,1)S(1)} %collective-permute-done.22.refs_4_) | copy-start | bytes 1572868
  97.3 12.1 %collective-permute-start.27 = (bf16[2,256,512]{2,1,0:T(8,128)(2,1)S(1)}, bf16[2,256,512]{2,1,0:T(8,128)(2,1)S(1)}, u32[]{:S(2)}, u32[]{:S(2)}) collective-permute-start(bf16[2,256,512]{2,1,0:T(8,128)(2,1)S(1)} %collective-permute-done.22.refs_4_), channel_id=1, source_target_pairs={{0,1},{1,0},{2,3},{3,2},{4,5},{5,4},{6,7},{7,6},{8,9},{9,8},{10,11... | collective-permute-start | bytes 1572872 | tf_op jit(solution)/shard_map/ppermute | solution.py:42
  101.6 13.6 %copy-start.20 = (bf16[2,256,512]{2,1,0:T(8,128)(2,1)}, bf16[2,256,512]{2,1,0:T(8,128)(2,1)S(1)}, u32[]{:S(2)}) copy-start(bf16[2,256,512]{2,1,0:T(8,128)(2,1)S(1)} %collective-permute-done.21.refs_3_) | copy-start | bytes 1572868
  101.6 7.9 %collective-permute-start.26 = (bf16[2,256,512]{2,1,0:T(8,128)(2,1)S(1)}, bf16[2,256,512]{2,1,0:T(8,128)(2,1)S(1)}, u32[]{:S(2)}, u32[]{:S(2)}) collective-permute-start(bf16[2,256,512]{2,1,0:T(8,128)(2,1)S(1)} %collective-permute-done.21.refs_3_), channel_id=1, source_target_pairs={{0,1},{1,0},{2,3},{3,2},{4,5},{5,4},{6,7},{7,6},{8,9},{9,8},{10,11... | collective-permute-start | bytes 1572872 | tf_op jit(solution)/shard_map/ppermute | solution.py:42
  103.9 11.4 %copy-start.14 = (bf16[4,256,512]{2,1,0:T(8,128)(2,1)}, bf16[4,256,512]{2,1,0:T(8,128)(2,1)S(1)}, u32[]{:S(2)}) copy-start(bf16[4,256,512]{2,1,0:T(8,128)(2,1)S(1)} %collective-permute-done.23.refs_5_) | copy-start | bytes 3145732
  103.9 26.3 %collective-permute-start.28 = (s16[608,128]{1,0:T(8,128)(2,1)}, s16[608,128]{1,0:T(8,128)(2,1)S(1)}, u32[]{:S(2)}, u32[]{:S(2)}) collective-permute-start(s16[608,128]{1,0:T(8,128)(2,1)} %get-tuple-element.20), channel_id=1, source_target_pairs={{128,0},{160,32},{192,64},{224,96},{0,128},{32,160},{64,192},{96,2... | collective-permute-start | bytes 466952 | tf_op jit(solution)/shard_map/ppermute | solution.py:37
  109.3 20.9 %collective-permute-start.29 = (s16[608,128]{1,0:T(8,128)(2,1)}, s16[608,128]{1,0:T(8,128)(2,1)S(1)}, u32[]{:S(2)}, u32[]{:S(2)}) collective-permute-start(s16[608,128]{1,0:T(8,128)(2,1)} %get-tuple-element.24), channel_id=1, source_target_pairs={{160,0},{192,32},{224,64},{0,96},{32,128},{64,160},{96,192},{128,2... | collective-permute-start | bytes 466952 | tf_op jit(solution)/shard_map/ppermute | solution.py:37
  109.5 23.6 %collective-permute-start.30 = (s16[608,128]{1,0:T(8,128)(2,1)}, s16[608,128]{1,0:T(8,128)(2,1)S(1)}, u32[]{:S(2)}, u32[]{:S(2)}) collective-permute-start(s16[608,128]{1,0:T(8,128)(2,1)} %get-tuple-element.25), channel_id=1, source_target_pairs={{96,0},{128,32},{160,64},{192,96},{224,128},{0,160},{32,192},{64,2... | collective-permute-start | bytes 466952 | tf_op jit(solution)/shard_map/ppermute | solution.py:37
  113.8 17.8 %copy-start.10 = (s32[4752]{0:T(1024)S(1)}, s32[4752]{0:T(1024)}, u32[]{:S(2)}) copy-start(s32[4752]{0:T(1024)} %param.10) | copy-start | bytes 57028
  113.8 18.0 %copy-start.6 = (s32[2048,8]{0,1:T(8,128)S(1)}, s32[2048,8]{0,1:T(8,128)}, u32[]{:S(2)}) copy-start(s32[2048,8]{0,1:T(8,128)} %param.11) | copy-start | bytes 196612
  113.8 19.2 %collective-permute-start.31 = (s16[608,128]{1,0:T(8,128)(2,1)}, s16[608,128]{1,0:T(8,128)(2,1)S(1)}, u32[]{:S(2)}, u32[]{:S(2)}) collective-permute-start(s16[608,128]{1,0:T(8,128)(2,1)} %get-tuple-element.26), channel_id=1, source_target_pairs={{192,0},{224,32},{0,64},{32,96},{64,128},{96,160},{128,192},{160,2... | collective-permute-start | bytes 466952 | tf_op jit(solution)/shard_map/ppermute | solution.py:37
  127.7 13.5 %copy-start.1 = (f32[608,128]{1,0:T(8,128)S(1)}, f32[608,128]{1,0:T(8,128)}, u32[]{:S(2)}) copy-start(f32[608,128]{1,0:T(8,128)} %get-tuple-element.23.own) | copy-start | bytes 933892
  127.7 9.5 %collective-permute-start.32 = (s16[608,128]{1,0:T(8,128)(2,1)}, s16[608,128]{1,0:T(8,128)(2,1)S(1)}, u32[]{:S(2)}, u32[]{:S(2)}) collective-permute-start(s16[608,128]{1,0:T(8,128)(2,1)} %get-tuple-element.27), channel_id=1, source_target_pairs={{64,0},{96,32},{128,64},{160,96},{192,128},{224,160},{0,192},{32,2... | collective-permute-start | bytes 466952 | tf_op jit(solution)/shard_map/ppermute | solution.py:37
  130.2 9.7 %collective-permute-start.33 = (s16[608,128]{1,0:T(8,128)(2,1)}, s16[608,128]{1,0:T(8,128)(2,1)S(1)}, u32[]{:S(2)}, u32[]{:S(2)}) collective-permute-start(s16[608,128]{1,0:T(8,128)(2,1)} %get-tuple-element.28), channel_id=1, source_target_pairs={{32,0},{64,32},{96,64},{128,96},{160,128},{192,160},{224,192},{0,2... | collective-permute-start | bytes 466952 | tf_op jit(solution)/shard_map/ppermute | solution.py:37
  130.2 10.3 %collective-permute-start.34 = (s16[608,128]{1,0:T(8,128)(2,1)}, s16[608,128]{1,0:T(8,128)(2,1)S(1)}, u32[]{:S(2)}, u32[]{:S(2)}) collective-permute-start(s16[608,128]{1,0:T(8,128)(2,1)} %get-tuple-element.29), channel_id=1, source_target_pairs={{224,0},{0,32},{32,64},{64,96},{96,128},{128,160},{160,192},{192,2... | collective-permute-start | bytes 466952 | tf_op jit(solution)/shard_map/ppermute | solution.py:37
  (10 other events, 19.3 us)
